TPU v7x, 512 devices: a whole 4x4x16 slice. The times are simulated.
512 devices in a mesh: gx: 32 (over y, x, core), gy: 16 (over z).
Axes of the slice: x: 4, y: 4, z: 16, core: 2. Of those that a mesh axis runs over, the one named last changes fastest.
Arguments:
- velocity: float32 [3, 512, 512, 256], P(None, 'gx', 'gy'), may hold values from -6 to 6
- refine_flags: int32 [3, 64, 64], P(None, 'gx', 'gy'), may hold values 0 or 1
- metric_table: float32 [3, 64], replicated, may hold values from 0.25 to 2.5
- index_x: int32 [512], P('gx'), may hold values from 0 to 63
- index_y: int32 [512], P('gy'), may hold values from 0 to 63
- index_z: int32 [256], replicated, may hold values from 0 to 63
Outputs:
- details_one: float32 [3, 7, 256, 256, 128], P(None, None, 'gx', 'gy')
- details_two: float32 [3, 7, 128, 128, 64], P(None, None, 'gx', 'gy')
- details_three: float32 [3, 7, 64, 64, 32], P(None, None, 'gx', 'gy')
- coarse: float32 [3, 64, 64, 32], P(None, 'gx', 'gy')
All inputs are finite; a program needn't handle non-finite values. No bound on the sum of `refine_flags` on one device may be relied on, other than what follows from the above.
Results may differ from a plain program's by a relative error of at most 0.00002.
Values sent between devices are 32-bit elements; how exact they have to be, the bound alone decides.
A program may use at most 64 MiB of HBM per device.

v0:
```python
import jax
import jax.numpy as jnp
from jax import lax
from jax.sharding import PartitionSpec as P

LEVELS = 3
BLOCK = 8


def padded_2(block, sides, width):
    for axis, dim in sides:
        count = lax.axis_size(axis)
        forward = [(i, i + 1) for i in range(count - 1)]
        forward.append((count - 1, 0))
        backward = [(target, source) for source, target in forward]
        low = lax.ppermute(
            lax.slice_in_dim(block, block.shape[dim] - width, None, axis=dim), axis, forward
        )
        high = lax.ppermute(lax.slice_in_dim(block, 0, width, axis=dim), axis, backward)
        block = jnp.concatenate([low, block, high], axis=dim)
    return block


def periodic_ext(values, axis_no, width):
    length = values.shape[axis_no]
    head_part = lax.slice_in_dim(values, length - width, length, axis=axis_no)
    tail_part = lax.slice_in_dim(values, 0, width, axis=axis_no)
    return jnp.concatenate([head_part, values, tail_part], axis=axis_no)


def central(extended, axis_no, length):
    return lax.slice_in_dim(extended, 2, length + 2, axis=axis_no) - lax.slice_in_dim(
        extended, 0, length, axis=axis_no
    )


def even_odd(values, axis_no):
    length = values.shape[axis_no]
    even_part = lax.slice_in_dim(values, 0, length, stride=2, axis=axis_no)
    odd_part = lax.slice_in_dim(values, 1, length, stride=2, axis=axis_no)
    return (even_part, odd_part)


def predict_step(even_ext, odd_part, axis_no, keep_mask):
    length = odd_part.shape[axis_no]
    left_one = lax.slice_in_dim(even_ext, 1, length + 1, axis=axis_no)
    centre = lax.slice_in_dim(even_ext, 2, length + 2, axis=axis_no)
    right_one = lax.slice_in_dim(even_ext, 3, length + 3, axis=axis_no)
    right_two = lax.slice_in_dim(even_ext, 4, length + 4, axis=axis_no)
    return (odd_part - (9.0 * (centre + right_one) - (left_one + right_two)) / 16.0) * keep_mask


def update_step(even_part, detail_ext, axis_no):
    length = even_part.shape[axis_no]
    left_two = lax.slice_in_dim(detail_ext, 0, length, axis=axis_no)
    left_one = lax.slice_in_dim(detail_ext, 1, length + 1, axis=axis_no)
    centre = lax.slice_in_dim(detail_ext, 2, length + 2, axis=axis_no)
    right_one = lax.slice_in_dim(detail_ext, 3, length + 3, axis=axis_no)
    return even_part + (9.0 * (left_one + centre) - (left_two + right_one)) / 32.0


def lift_local(values, axis_no, keep_mask):
    even_part, odd_part = even_odd(values, axis_no)
    detail = predict_step(periodic_ext(even_part, axis_no, 2), odd_part, axis_no, keep_mask)
    smooth = update_step(even_part, periodic_ext(detail, axis_no, 2), axis_no)
    return (smooth, detail)


def level_mask(flag_plane, rep_x, rep_y):
    return jnp.repeat(jnp.repeat(flag_plane, rep_x, axis=0), rep_y, axis=1).astype(jnp.float32)


def lift_along_x(values, plane_x):
    even_part, odd_part = even_odd(values, 1)
    even_ext = padded_2(even_part, (("gx", 1),), 2)
    detail = predict_step(even_ext, odd_part, 1, plane_x[None, :, :, None])
    detail_ext = padded_2(detail, (("gx", 1),), 2)
    return (update_step(even_part, detail_ext, 1), detail)


def lift_along_y(values, plane_yz):
    even_part, odd_part = even_odd(values, 3)
    even_ext = padded_2(even_part, (("gy", 3),), 2)
    detail = predict_step(even_ext, odd_part, 3, plane_yz[None, None, :, :, None])
    detail_ext = padded_2(detail, (("gy", 3),), 2)
    return (update_step(even_part, detail_ext, 3), detail)


def on_device(velocity, refine_flags, metric_table, index_x, index_y, index_z):
    classes_no = metric_table.shape[1]
    class_ids = jnp.arange(classes_no, dtype=jnp.int32)

    def lookup(row_no, line_ids):
        onehot = (line_ids[:, None] == class_ids[None, :]).astype(jnp.float32)
        return jnp.sum(onehot * metric_table[row_no][None, :], axis=1)

    metric_x = lookup(0, index_x)[:, None, None]
    metric_y = lookup(1, index_y)[None, :, None]
    metric_z = lookup(2, index_z)[None, None, None, :]
    width_x = velocity.shape[1]
    width_y = velocity.shape[2]
    depth_z = velocity.shape[3]
    padded = padded_2(velocity, (("gx", 1), ("gy", 2)), 1)
    diff_x = central(padded[:, :, 1:-1], 1, width_x)
    diff_y = central(padded[:, 1:-1], 2, width_y)
    dv_dx = diff_x[1] * metric_x
    dw_dx = diff_x[2] * metric_x
    du_dy = diff_y[0] * metric_y
    dw_dy = diff_y[2] * metric_y
    diff_z = central(periodic_ext(velocity, 3, 1), 3, depth_z) * metric_z
    vort_x = dw_dy - diff_z[1]
    vort_y = diff_z[0] - dw_dx
    vort_z = dv_dx - du_dy
    current = jnp.stack([vort_x, vort_y, vort_z])
    results = []
    for level_idx in range(LEVELS):
        repeat_no = BLOCK // 2 ** (level_idx + 1)
        flag_plane = refine_flags[level_idx]
        plane_x = level_mask(flag_plane, repeat_no, 2 * repeat_no)
        plane_yz = level_mask(flag_plane, repeat_no, repeat_no)
        if level_idx < LEVELS - 1:
            smooth, detail = lift_along_x(current, plane_x)
            halfway = jnp.stack([smooth, detail], axis=1)
            smooth, detail = lift_along_y(halfway, plane_yz)
        else:
            smooth, detail = lift_along_x(current, plane_x)
            halfway = jnp.stack([smooth, detail], axis=1)
            smooth, detail = lift_along_y(halfway, plane_yz)
        halfway = jnp.stack([smooth, detail], axis=2)
        smooth, detail = lift_local(halfway, 5, plane_yz[None, None, None, :, :, None])
        stacked = jnp.stack([smooth, detail], axis=3)
        bands = stacked.reshape((3, 8) + stacked.shape[4:])
        results.append(bands[:, 1:])
        current = bands[:, 0]
    return (results[0], results[1], results[2], current)


def solution(mesh):
    return jax.shard_map(
        on_device,
        mesh=mesh,
        in_specs=(P(None, "gx", "gy", None), P(None, "gx", "gy"), P(), P("gx"), P("gy"), P()),
        out_specs=(
            P(None, None, "gx", "gy", None),
            P(None, None, "gx", "gy", None),
            P(None, None, "gx", "gy", None),
            P(None, "gx", "gy", None),
        ),
        check_vma=False,
    )
```

profile of v0, /device:TPU:31, one launch (start us, length us, event | category | flops | bytes accessed | tf_op | source)
XLA Modules:
  0.0 241.9 jit_solution(18323125442558814479)
XLA Ops:
  1.6 7.7 %collective-permute-start = (f32[3,1,32,256]{3,2,1,0:T(8,128)S(1)}, f32[3,1,32,256]{3,2,1,0:T(8,128)S(1)}, u32[]{:S(2)}, u32[]{:S(2)}) collective-permute-start(f32[3,1,32,256]{3,2,1,0:T(8,128)S(1)} %get-tuple-element.25), channel_id=1, source_target_pairs={{0,16},{16,32},{32,48},{48,64},{64,80},{80,96},{96,112},{112,128},... | collective-permute-start | bytes 294920 | tf_op jit(solution)/shard_map/ppermute | solution.py:16
  9.3 2.1 collective-permute-start.1
  14.8 3.9 %collective-permute-done.1 = f32[3,1,32,256]{3,2,1,0:T(8,128)S(1)} collective-permute-done((f32[3,1,32,256]{3,2,1,0:T(8,128)S(1)}, f32[3,1,32,256]{3,2,1,0:T(8,128)S(1)}, u32[]{:S(2)}, u32[]{:S(2)}) %collective-permute-start.1) | collective-permute-done | bytes 98336 | tf_op jit(solution)/shard_map/ppermute | solution.py:19
  18.8 5.8 %collective-permute-start.2 = (f32[3,18,1,256]{3,2,1,0:T(1,128)S(1)}, f32[3,18,1,256]{3,2,1,0:T(1,128)S(1)}, u32[]{:S(2)}, u32[]{:S(2)}) collective-permute-start(f32[3,18,1,256]{3,2,1,0:T(1,128)S(1)} %get-tuple-element.19), channel_id=1, source_target_pairs={{1,0},{2,1},{3,2},{4,3},{5,4},{6,5},{7,6},{8,7},{9,8},{10,9},{11,1... | collective-permute-start | bytes 165896 | tf_op jit(solution)/shard_map/ppermute | solution.py:19
  24.6 1.9 collective-permute-start.3
  26.7 4.0 %collective-permute-done.3 = f32[3,18,1,256]{3,2,1,0:T(1,128)S(1)} collective-permute-done((f32[3,18,1,256]{3,2,1,0:T(1,128)S(1)}, f32[3,18,1,256]{3,2,1,0:T(1,128)S(1)}, u32[]{:S(2)}, u32[]{:S(2)}) %collective-permute-start.3) | collective-permute-done | bytes 55328 | tf_op jit(solution)/shard_map/ppermute | solution.py:16
  31.4 1.9 collective-permute-start.4
  33.3 7.0 %collective-permute-start.5 = (f32[3,2,32,256]{3,2,1,0:T(8,128)S(1)}, f32[3,2,32,256]{3,2,1,0:T(8,128)S(1)}, u32[]{:S(2)}, u32[]{:S(2)}) collective-permute-start(f32[3,2,32,256]{3,2,1,0:T(8,128)S(1)} %get-tuple-element.36), channel_id=1, source_target_pairs={{0,16},{16,32},{32,48},{48,64},{64,80},{80,96},{96,112},{112,128},... | collective-permute-start | bytes 589832 | tf_op jit(solution)/shard_map/ppermute | solution.py:16
  43.1 7.7 %collective-permute-start.6 = (f32[3,2,32,256]{3,2,1,0:T(8,128)S(1)}, f32[3,2,32,256]{3,2,1,0:T(8,128)S(1)}, u32[]{:S(2)}, u32[]{:S(2)}) collective-permute-start(f32[3,2,32,256]{3,2,1,0:T(8,128)S(1)} %get-tuple-element.35), channel_id=1, source_target_pairs={{0,16},{16,32},{32,48},{48,64},{64,80},{80,96},{96,112},{112,128},... | collective-permute-start | bytes 589832 | tf_op jit(solution)/shard_map/ppermute | solution.py:16
  50.8 1.9 collective-permute-start.7
  53.4 7.7 %collective-permute-done.7 = f32[3,2,32,256]{3,2,1,0:T(8,128)S(1)} collective-permute-done((f32[3,2,32,256]{3,2,1,0:T(8,128)S(1)}, f32[3,2,32,256]{3,2,1,0:T(8,128)S(1)}, u32[]{:S(2)}, u32[]{:S(2)}) %collective-permute-start.7) | collective-permute-done | bytes 196640 | tf_op jit(solution)/shard_map/ppermute | solution.py:19
  62.1 1.9 collective-permute-start.8
  64.0 3.4 %collective-permute-start.9 = (f32[3,2,8,2,256]{4,3,2,0,1:T(2,128)S(1)}, f32[3,2,8,2,256]{4,3,2,0,1:T(2,128)S(1)}, u32[]{:S(2)}, u32[]{:S(2)}) collective-permute-start(f32[3,2,8,2,256]{4,3,2,0,1:T(2,128)S(1)} %get-tuple-element.32), channel_id=1, source_target_pairs={{0,1},{1,2},{2,3},{3,4},{4,5},{5,6},{6,7},{7,8},{8,9},{9,10},{10,1... | collective-permute-start | bytes 294920 | tf_op jit(solution)/shard_map/ppermute | solution.py:16
  68.0 2.6 %collective-permute-done.9 = f32[3,2,8,2,256]{4,3,2,0,1:T(2,128)S(1)} collective-permute-done((f32[3,2,8,2,256]{4,3,2,0,1:T(2,128)S(1)}, f32[3,2,8,2,256]{4,3,2,0,1:T(2,128)S(1)}, u32[]{:S(2)}, u32[]{:S(2)}) %collective-permute-start.9) | collective-permute-done | bytes 98336 | tf_op jit(solution)/shard_map/ppermute | solution.py:16
  71.2 2.6 %collective-permute-start.10 = (f32[3,2,8,2,256]{4,3,2,0,1:T(2,128)S(1)}, f32[3,2,8,2,256]{4,3,2,0,1:T(2,128)S(1)}, u32[]{:S(2)}, u32[]{:S(2)}) collective-permute-start(f32[3,2,8,2,256]{4,3,2,0,1:T(2,128)S(1)} %get-tuple-element.31), channel_id=1, source_target_pairs={{0,1},{1,2},{2,3},{3,4},{4,5},{5,6},{6,7},{7,8},{8,9},{9,10},{10,1... | collective-permute-start | bytes 294920 | tf_op jit(solution)/shard_map/ppermute | solution.py:16
  73.8 3.9 %collective-permute-start.11 = (f32[3,2,8,2,256]{4,3,2,0,1:T(2,128)S(1)}, f32[3,2,8,2,256]{4,3,2,0,1:T(2,128)S(1)}, u32[]{:S(2)}, u32[]{:S(2)}) collective-permute-start(f32[3,2,8,2,256]{4,3,2,0,1:T(2,128)S(1)} %get-tuple-element.30), channel_id=1, source_target_pairs={{1,0},{2,1},{3,2},{4,3},{5,4},{6,5},{7,6},{8,7},{9,8},{10,9},{11,1... | collective-permute-start | bytes 294920 | tf_op jit(solution)/shard_map/ppermute | solution.py:19
  79.9 26.8 %slice.503 = f32[3,2,2,8,16,128]{5,4,3,0,1,2:T(8,128)S(1)} slice(f32[3,2,2,8,16,256]{5,4,3,0,1,2:T(8,128)S(1)} %pad_maximum_fusion.4), slice={[0:3:1], [0:2:1], [0:2:1], [0:8:1], [0:16:1], [0:256:2]} | slice | bytes 1572864 | tf_op jit(solution)/shard_map/slice | solution.py:39
  106.7 26.8 %slice.504 = f32[3,2,2,8,16,128]{5,4,3,0,1,2:T(8,128)S(1)} slice(f32[3,2,2,8,16,256]{5,4,3,0,1,2:T(8,128)S(1)} %pad_maximum_fusion.4), slice={[0:3:1], [0:2:1], [0:2:1], [0:8:1], [0:16:1], [1:256:2]} | slice | bytes 1572864 | tf_op jit(solution)/shard_map/slice | solution.py:40
  138.8 7.0 %collective-permute-start.13 = (f32[3,2,16,128]{3,2,1,0:T(8,128)S(1)}, f32[3,2,16,128]{3,2,1,0:T(8,128)S(1)}, u32[]{:S(2)}, u32[]{:S(2)}) collective-permute-start(f32[3,2,16,128]{3,2,1,0:T(8,128)S(1)} %get-tuple-element.48), channel_id=1, source_target_pairs={{0,16},{16,32},{32,48},{48,64},{64,80},{80,96},{96,112},{112,128},... | collective-permute-start | bytes 147464 | tf_op jit(solution)/shard_map/ppermute | solution.py:16
  147.0 7.7 %collective-permute-start.14 = (f32[3,2,16,128]{3,2,1,0:T(8,128)S(1)}, f32[3,2,16,128]{3,2,1,0:T(8,128)S(1)}, u32[]{:S(2)}, u32[]{:S(2)}) collective-permute-start(f32[3,2,16,128]{3,2,1,0:T(8,128)S(1)} %get-tuple-element.47), channel_id=1, source_target_pairs={{0,16},{16,32},{32,48},{48,64},{64,80},{80,96},{96,112},{112,128},... | collective-permute-start | bytes 147464 | tf_op jit(solution)/shard_map/ppermute | solution.py:16
  156.7 6.8 %collective-permute-done.15 = f32[3,2,16,128]{3,2,1,0:T(8,128)S(1)} collective-permute-done((f32[3,2,16,128]{3,2,1,0:T(8,128)S(1)}, f32[3,2,16,128]{3,2,1,0:T(8,128)S(1)}, u32[]{:S(2)}, u32[]{:S(2)}) %collective-permute-start.15) | collective-permute-done | bytes 49184 | tf_op jit(solution)/shard_map/ppermute | solution.py:19
  163.7 4.9 %collective-permute-start.16 = (f32[3,2,4,2,128]{4,3,2,0,1:T(2,128)S(1)}, f32[3,2,4,2,128]{4,3,2,0,1:T(2,128)S(1)}, u32[]{:S(2)}, u32[]{:S(2)}) collective-permute-start(f32[3,2,4,2,128]{4,3,2,0,1:T(2,128)S(1)} %get-tuple-element.45), channel_id=1, source_target_pairs={{1,0},{2,1},{3,2},{4,3},{5,4},{6,5},{7,6},{8,7},{9,8},{10,9},{11,1... | collective-permute-start | bytes 73736 | tf_op jit(solution)/shard_map/ppermute | solution.py:19
  170.9 3.5 %collective-permute-done.17 = f32[3,2,4,2,128]{4,3,2,0,1:T(2,128)S(1)} collective-permute-done((f32[3,2,4,2,128]{4,3,2,0,1:T(2,128)S(1)}, f32[3,2,4,2,128]{4,3,2,0,1:T(2,128)S(1)}, u32[]{:S(2)}, u32[]{:S(2)}) %collective-permute-start.17) | collective-permute-done | bytes 24608 | tf_op jit(solution)/shard_map/ppermute | solution.py:16
  176.5 4.6 %collective-permute-start.19 = (f32[3,2,4,2,128]{4,3,2,0,1:T(2,128)S(1)}, f32[3,2,4,2,128]{4,3,2,0,1:T(2,128)S(1)}, u32[]{:S(2)}, u32[]{:S(2)}) collective-permute-start(f32[3,2,4,2,128]{4,3,2,0,1:T(2,128)S(1)} %get-tuple-element.42), channel_id=1, source_target_pairs={{1,0},{2,1},{3,2},{4,3},{5,4},{6,5},{7,6},{8,7},{9,8},{10,9},{11,1... | collective-permute-start | bytes 73736 | tf_op jit(solution)/shard_map/ppermute | solution.py:19
  182.1 4.2 %slice.542 = f32[3,2,2,4,8,64]{5,4,3,0,1,2:T(8,128)S(1)} slice(f32[3,2,2,4,8,128]{5,4,3,0,1,2:T(8,128)S(1)} %pad_maximum_fusion.28), slice={[0:3:1], [0:2:1], [0:2:1], [0:4:1], [0:8:1], [0:128:2]} | slice | bytes 196608 | tf_op jit(solution)/shard_map/slice | solution.py:39
  186.4 4.3 %slice.543 = f32[3,2,2,4,8,64]{5,4,3,0,1,2:T(8,128)S(1)} slice(f32[3,2,2,4,8,128]{5,4,3,0,1,2:T(8,128)S(1)} %pad_maximum_fusion.28), slice={[0:3:1], [0:2:1], [0:2:1], [0:4:1], [0:8:1], [1:128:2]} | slice | bytes 196608 | tf_op jit(solution)/shard_map/slice | solution.py:40
  193.6 7.0 %collective-permute-start.21 = (f32[3,2,8,64]{3,2,1,0:T(8,128)S(1)}, f32[3,2,8,64]{3,2,1,0:T(8,128)S(1)}, u32[]{:S(2)}, u32[]{:S(2)}) collective-permute-start(f32[3,2,8,64]{3,2,1,0:T(8,128)S(1)} %slice.556), channel_id=1, source_target_pairs={{0,16},{16,32},{32,48},{48,64},{64,80},{80,96},{96,112},{112,128},... | collective-permute-start | bytes 36872 | tf_op jit(solution)/shard_map/ppermute | solution.py:16
  201.6 7.5 %collective-permute-start.22 = (f32[3,2,8,64]{3,2,1,0:T(8,128)S(1)}, f32[3,2,8,64]{3,2,1,0:T(8,128)S(1)}, u32[]{:S(2)}, u32[]{:S(2)}) collective-permute-start(f32[3,2,8,64]{3,2,1,0:T(8,128)S(1)} %fusion.139), channel_id=1, source_target_pairs={{0,16},{16,32},{32,48},{48,64},{64,80},{80,96},{96,112},{112,128},... | collective-permute-start | bytes 36872 | tf_op jit(solution)/shard_map/ppermute | solution.py:16
  211.1 6.5 %collective-permute-done.23 = f32[3,2,8,64]{3,2,1,0:T(8,128)S(1)} collective-permute-done((f32[3,2,8,64]{3,2,1,0:T(8,128)S(1)}, f32[3,2,8,64]{3,2,1,0:T(8,128)S(1)}, u32[]{:S(2)}, u32[]{:S(2)}) %collective-permute-start.23) | collective-permute-done | bytes 12320 | tf_op jit(solution)/shard_map/ppermute | solution.py:19
  217.8 4.8 %collective-permute-start.24 = (f32[3,2,2,2,64]{4,3,2,0,1:T(2,128)S(1)}, f32[3,2,2,2,64]{4,3,2,0,1:T(2,128)S(1)}, u32[]{:S(2)}, u32[]{:S(2)}) collective-permute-start(f32[3,2,2,2,64]{4,3,2,0,1:T(2,128)S(1)} %get-tuple-element.57), channel_id=1, source_target_pairs={{1,0},{2,1},{3,2},{4,3},{5,4},{6,5},{7,6},{8,7},{9,8},{10,9},{11,1... | collective-permute-start | bytes 18440 | tf_op jit(solution)/shard_map/ppermute | solution.py:19
  224.8 3.5 %collective-permute-done.25 = f32[3,2,2,2,64]{4,3,2,0,1:T(2,128)S(1)} collective-permute-done((f32[3,2,2,2,64]{4,3,2,0,1:T(2,128)S(1)}, f32[3,2,2,2,64]{4,3,2,0,1:T(2,128)S(1)}, u32[]{:S(2)}, u32[]{:S(2)}) %collective-permute-start.25) | collective-permute-done | bytes 6176 | tf_op jit(solution)/shard_map/ppermute | solution.py:16
  230.4 4.6 %collective-permute-start.27 = (f32[3,2,2,2,64]{4,3,2,0,1:T(2,128)S(1)}, f32[3,2,2,2,64]{4,3,2,0,1:T(2,128)S(1)}, u32[]{:S(2)}, u32[]{:S(2)}) collective-permute-start(f32[3,2,2,2,64]{4,3,2,0,1:T(2,128)S(1)} %get-tuple-element.54), channel_id=1, source_target_pairs={{1,0},{2,1},{3,2},{4,3},{5,4},{6,5},{7,6},{8,7},{9,8},{10,9},{11,1... | collective-permute-start | bytes 18440 | tf_op jit(solution)/shard_map/ppermute | solution.py:19
  (134 shorter events, 43.8 us)
Async XLA Ops:
  1.6 12.0 %collective-permute-start = (f32[3,1,32,256]{3,2,1,0:T(8,128)S(1)}, f32[3,1,32,256]{3,2,1,0:T(8,128)S(1)}, u32[]{:S(2)}, u32[]{:S(2)}) collective-permute-start(f32[3,1,32,256]{3,2,1,0:T(8,128)S(1)} %get-tuple-element.25), channel_id=1, source_target_pairs={{0,16},{16,32},{32,48},{48,64},{64,80},{80,96},{96,112},{112,128},... | collective-permute-start | bytes 294920 | tf_op jit(solution)/shard_map/ppermute | solution.py:16
  9.3 3.9 %copy-start.4 = (s32[16]{0:T(128)S(1)}, s32[16]{0:T(128)}, u32[]{:S(2)}) copy-start(s32[16]{0:T(128)} %param.9) | copy-start | bytes 196
  9.3 4.1 %copy-start.5 = (s32[32]{0:T(128)S(1)}, s32[32]{0:T(128)}, u32[]{:S(2)}) copy-start(s32[32]{0:T(128)} %param.10) | copy-start | bytes 388
  9.3 4.3 %copy-start = (f32[3,16,32,256]{3,2,1,0:T(8,128)S(1)}, f32[3,16,32,256]{3,2,1,0:T(8,128)}, u32[]{:S(2)}) copy-start(f32[3,16,32,256]{3,2,1,0:T(8,128)} %param.6) | copy-start | bytes 4718596
  9.3 9.4 %collective-permute-start.1 = (f32[3,1,32,256]{3,2,1,0:T(8,128)S(1)}, f32[3,1,32,256]{3,2,1,0:T(8,128)S(1)}, u32[]{:S(2)}, u32[]{:S(2)}) collective-permute-start(f32[3,1,32,256]{3,2,1,0:T(8,128)S(1)} %get-tuple-element.24), channel_id=1, source_target_pairs={{16,0},{32,16},{48,32},{64,48},{80,64},{96,80},{112,96},{128,112},... | collective-permute-start | bytes 294920 | tf_op jit(solution)/shard_map/ppermute | solution.py:19
  18.8 7.9 %collective-permute-start.2 = (f32[3,18,1,256]{3,2,1,0:T(1,128)S(1)}, f32[3,18,1,256]{3,2,1,0:T(1,128)S(1)}, u32[]{:S(2)}, u32[]{:S(2)}) collective-permute-start(f32[3,18,1,256]{3,2,1,0:T(1,128)S(1)} %get-tuple-element.19), channel_id=1, source_target_pairs={{1,0},{2,1},{3,2},{4,3},{5,4},{6,5},{7,6},{8,7},{9,8},{10,9},{11,1... | collective-permute-start | bytes 165896 | tf_op jit(solution)/shard_map/ppermute | solution.py:19
  24.6 6.1 %collective-permute-start.3 = (f32[3,18,1,256]{3,2,1,0:T(1,128)S(1)}, f32[3,18,1,256]{3,2,1,0:T(1,128)S(1)}, u32[]{:S(2)}, u32[]{:S(2)}) collective-permute-start(f32[3,18,1,256]{3,2,1,0:T(1,128)S(1)} %get-tuple-element.18), channel_id=1, source_target_pairs={{0,1},{1,2},{2,3},{3,4},{4,5},{5,6},{6,7},{7,8},{8,9},{9,10},{10,1... | collective-permute-start | bytes 165896 | tf_op jit(solution)/shard_map/ppermute | solution.py:16
  31.2 9.0 %copy-start.1 = (s32[3,2,4]{2,1,0:T(2,128)S(1)}, s32[3,2,4]{2,1,0:T(2,128)}, u32[]{:S(2)}) copy-start(s32[3,2,4]{2,1,0:T(2,128)} %param.7) | copy-start | bytes 292
  31.4 10.3 %collective-permute-start.4 = (f32[3,2,32,256]{3,2,1,0:T(8,128)S(1)}, f32[3,2,32,256]{3,2,1,0:T(8,128)S(1)}, u32[]{:S(2)}, u32[]{:S(2)}) collective-permute-start(f32[3,2,32,256]{3,2,1,0:T(8,128)S(1)} %get-tuple-element.37), channel_id=1, source_target_pairs={{16,0},{32,16},{48,32},{64,48},{80,64},{96,80},{112,96},{128,112},... | collective-permute-start | bytes 589832 | tf_op jit(solution)/shard_map/ppermute | solution.py:19
  33.3 9.6 %collective-permute-start.5 = (f32[3,2,32,256]{3,2,1,0:T(8,128)S(1)}, f32[3,2,32,256]{3,2,1,0:T(8,128)S(1)}, u32[]{:S(2)}, u32[]{:S(2)}) collective-permute-start(f32[3,2,32,256]{3,2,1,0:T(8,128)S(1)} %get-tuple-element.36), channel_id=1, source_target_pairs={{0,16},{16,32},{32,48},{48,64},{64,80},{80,96},{96,112},{112,128},... | collective-permute-start | bytes 589832 | tf_op jit(solution)/shard_map/ppermute | solution.py:16
  43.1 10.3 %collective-permute-start.6 = (f32[3,2,32,256]{3,2,1,0:T(8,128)S(1)}, f32[3,2,32,256]{3,2,1,0:T(8,128)S(1)}, u32[]{:S(2)}, u32[]{:S(2)}) collective-permute-start(f32[3,2,32,256]{3,2,1,0:T(8,128)S(1)} %get-tuple-element.35), channel_id=1, source_target_pairs={{0,16},{16,32},{32,48},{48,64},{64,80},{80,96},{96,112},{112,128},... | collective-permute-start | bytes 589832 | tf_op jit(solution)/shard_map/ppermute | solution.py:16
  50.8 10.3 %collective-permute-start.7 = (f32[3,2,32,256]{3,2,1,0:T(8,128)S(1)}, f32[3,2,32,256]{3,2,1,0:T(8,128)S(1)}, u32[]{:S(2)}, u32[]{:S(2)}) collective-permute-start(f32[3,2,32,256]{3,2,1,0:T(8,128)S(1)} %get-tuple-element.34), channel_id=1, source_target_pairs={{16,0},{32,16},{48,32},{64,48},{80,64},{96,80},{112,96},{128,112},... | collective-permute-start | bytes 589832 | tf_op jit(solution)/shard_map/ppermute | solution.py:19
  62.1 5.9 %collective-permute-start.8 = (f32[3,2,8,2,256]{4,3,2,0,1:T(2,128)S(1)}, f32[3,2,8,2,256]{4,3,2,0,1:T(2,128)S(1)}, u32[]{:S(2)}, u32[]{:S(2)}) collective-permute-start(f32[3,2,8,2,256]{4,3,2,0,1:T(2,128)S(1)} %get-tuple-element.33), channel_id=1, source_target_pairs={{1,0},{2,1},{3,2},{4,3},{5,4},{6,5},{7,6},{8,7},{9,8},{10,9},{11,1... | collective-permute-start | bytes 294920 | tf_op jit(solution)/shard_map/ppermute | solution.py:19
  64.0 6.6 %collective-permute-start.9 = (f32[3,2,8,2,256]{4,3,2,0,1:T(2,128)S(1)}, f32[3,2,8,2,256]{4,3,2,0,1:T(2,128)S(1)}, u32[]{:S(2)}, u32[]{:S(2)}) collective-permute-start(f32[3,2,8,2,256]{4,3,2,0,1:T(2,128)S(1)} %get-tuple-element.32), channel_id=1, source_target_pairs={{0,1},{1,2},{2,3},{3,4},{4,5},{5,6},{6,7},{7,8},{8,9},{9,10},{10,1... | collective-permute-start | bytes 294920 | tf_op jit(solution)/shard_map/ppermute | solution.py:16
  71.2 6.6 %collective-permute-start.10 = (f32[3,2,8,2,256]{4,3,2,0,1:T(2,128)S(1)}, f32[3,2,8,2,256]{4,3,2,0,1:T(2,128)S(1)}, u32[]{:S(2)}, u32[]{:S(2)}) collective-permute-start(f32[3,2,8,2,256]{4,3,2,0,1:T(2,128)S(1)} %get-tuple-element.31), channel_id=1, source_target_pairs={{0,1},{1,2},{2,3},{3,4},{4,5},{5,6},{6,7},{7,8},{8,9},{9,10},{10,1... | collective-permute-start | bytes 294920 | tf_op jit(solution)/shard_map/ppermute | solution.py:16
  73.8 5.5 %collective-permute-start.11 = (f32[3,2,8,2,256]{4,3,2,0,1:T(2,128)S(1)}, f32[3,2,8,2,256]{4,3,2,0,1:T(2,128)S(1)}, u32[]{:S(2)}, u32[]{:S(2)}) collective-permute-start(f32[3,2,8,2,256]{4,3,2,0,1:T(2,128)S(1)} %get-tuple-element.30), channel_id=1, source_target_pairs={{1,0},{2,1},{3,2},{4,3},{5,4},{6,5},{7,6},{8,7},{9,8},{10,9},{11,1... | collective-permute-start | bytes 294920 | tf_op jit(solution)/shard_map/ppermute | solution.py:19
  136.8 9.1 %collective-permute-start.12 = (f32[3,2,16,128]{3,2,1,0:T(8,128)S(1)}, f32[3,2,16,128]{3,2,1,0:T(8,128)S(1)}, u32[]{:S(2)}, u32[]{:S(2)}) collective-permute-start(f32[3,2,16,128]{3,2,1,0:T(8,128)S(1)} %get-tuple-element.49), channel_id=1, source_target_pairs={{16,0},{32,16},{48,32},{64,48},{80,64},{96,80},{112,96},{128,112},... | collective-permute-start | bytes 147464 | tf_op jit(solution)/shard_map/ppermute | solution.py:19
  138.8 8.1 %collective-permute-start.13 = (f32[3,2,16,128]{3,2,1,0:T(8,128)S(1)}, f32[3,2,16,128]{3,2,1,0:T(8,128)S(1)}, u32[]{:S(2)}, u32[]{:S(2)}) collective-permute-start(f32[3,2,16,128]{3,2,1,0:T(8,128)S(1)} %get-tuple-element.48), channel_id=1, source_target_pairs={{0,16},{16,32},{32,48},{48,64},{64,80},{80,96},{96,112},{112,128},... | collective-permute-start | bytes 147464 | tf_op jit(solution)/shard_map/ppermute | solution.py:16
  147.0 9.7 %collective-permute-start.14 = (f32[3,2,16,128]{3,2,1,0:T(8,128)S(1)}, f32[3,2,16,128]{3,2,1,0:T(8,128)S(1)}, u32[]{:S(2)}, u32[]{:S(2)}) collective-permute-start(f32[3,2,16,128]{3,2,1,0:T(8,128)S(1)} %get-tuple-element.47), channel_id=1, source_target_pairs={{0,16},{16,32},{32,48},{48,64},{64,80},{80,96},{96,112},{112,128},... | collective-permute-start | bytes 147464 | tf_op jit(solution)/shard_map/ppermute | solution.py:16
  154.7 8.7 %collective-permute-start.15 = (f32[3,2,16,128]{3,2,1,0:T(8,128)S(1)}, f32[3,2,16,128]{3,2,1,0:T(8,128)S(1)}, u32[]{:S(2)}, u32[]{:S(2)}) collective-permute-start(f32[3,2,16,128]{3,2,1,0:T(8,128)S(1)} %get-tuple-element.46), channel_id=1, source_target_pairs={{16,0},{32,16},{48,32},{64,48},{80,64},{96,80},{112,96},{128,112},... | collective-permute-start | bytes 147464 | tf_op jit(solution)/shard_map/ppermute | solution.py:19
  163.7 7.2 %collective-permute-start.16 = (f32[3,2,4,2,128]{4,3,2,0,1:T(2,128)S(1)}, f32[3,2,4,2,128]{4,3,2,0,1:T(2,128)S(1)}, u32[]{:S(2)}, u32[]{:S(2)}) collective-permute-start(f32[3,2,4,2,128]{4,3,2,0,1:T(2,128)S(1)} %get-tuple-element.45), channel_id=1, source_target_pairs={{1,0},{2,1},{3,2},{4,3},{5,4},{6,5},{7,6},{8,7},{9,8},{10,9},{11,1... | collective-permute-start | bytes 73736 | tf_op jit(solution)/shard_map/ppermute | solution.py:19
  168.7 5.8 %collective-permute-start.17 = (f32[3,2,4,2,128]{4,3,2,0,1:T(2,128)S(1)}, f32[3,2,4,2,128]{4,3,2,0,1:T(2,128)S(1)}, u32[]{:S(2)}, u32[]{:S(2)}) collective-permute-start(f32[3,2,4,2,128]{4,3,2,0,1:T(2,128)S(1)} %get-tuple-element.44), channel_id=1, source_target_pairs={{0,1},{1,2},{2,3},{3,4},{4,5},{5,6},{6,7},{7,8},{8,9},{9,10},{10,1... | collective-permute-start | bytes 73736 | tf_op jit(solution)/shard_map/ppermute | solution.py:16
  174.6 6.5 %collective-permute-start.18 = (f32[3,2,4,2,128]{4,3,2,0,1:T(2,128)S(1)}, f32[3,2,4,2,128]{4,3,2,0,1:T(2,128)S(1)}, u32[]{:S(2)}, u32[]{:S(2)}) collective-permute-start(f32[3,2,4,2,128]{4,3,2,0,1:T(2,128)S(1)} %get-tuple-element.43), channel_id=1, source_target_pairs={{0,1},{1,2},{2,3},{3,4},{4,5},{5,6},{6,7},{7,8},{8,9},{9,10},{10,1... | collective-permute-start | bytes 73736 | tf_op jit(solution)/shard_map/ppermute | solution.py:16
  176.5 5.5 %collective-permute-start.19 = (f32[3,2,4,2,128]{4,3,2,0,1:T(2,128)S(1)}, f32[3,2,4,2,128]{4,3,2,0,1:T(2,128)S(1)}, u32[]{:S(2)}, u32[]{:S(2)}) collective-permute-start(f32[3,2,4,2,128]{4,3,2,0,1:T(2,128)S(1)} %get-tuple-element.42), channel_id=1, source_target_pairs={{1,0},{2,1},{3,2},{4,3},{5,4},{6,5},{7,6},{8,7},{9,8},{10,9},{11,1... | collective-permute-start | bytes 73736 | tf_op jit(solution)/shard_map/ppermute | solution.py:19
  191.7 9.1 %collective-permute-start.20 = (f32[3,2,8,64]{3,2,1,0:T(8,128)S(1)}, f32[3,2,8,64]{3,2,1,0:T(8,128)S(1)}, u32[]{:S(2)}, u32[]{:S(2)}) collective-permute-start(f32[3,2,8,64]{3,2,1,0:T(8,128)S(1)} %slice.556), channel_id=1, source_target_pairs={{16,0},{32,16},{48,32},{64,48},{80,64},{96,80},{112,96},{128,112},... | collective-permute-start | bytes 36872 | tf_op jit(solution)/shard_map/ppermute | solution.py:19
  193.6 7.9 %collective-permute-start.21 = (f32[3,2,8,64]{3,2,1,0:T(8,128)S(1)}, f32[3,2,8,64]{3,2,1,0:T(8,128)S(1)}, u32[]{:S(2)}, u32[]{:S(2)}) collective-permute-start(f32[3,2,8,64]{3,2,1,0:T(8,128)S(1)} %slice.556), channel_id=1, source_target_pairs={{0,16},{16,32},{32,48},{48,64},{64,80},{80,96},{96,112},{112,128},... | collective-permute-start | bytes 36872 | tf_op jit(solution)/shard_map/ppermute | solution.py:16
  201.6 9.5 %collective-permute-start.22 = (f32[3,2,8,64]{3,2,1,0:T(8,128)S(1)}, f32[3,2,8,64]{3,2,1,0:T(8,128)S(1)}, u32[]{:S(2)}, u32[]{:S(2)}) collective-permute-start(f32[3,2,8,64]{3,2,1,0:T(8,128)S(1)} %fusion.139), channel_id=1, source_target_pairs={{0,16},{16,32},{32,48},{48,64},{64,80},{80,96},{96,112},{112,128},... | collective-permute-start | bytes 36872 | tf_op jit(solution)/shard_map/ppermute | solution.py:16
  209.1 8.5 %collective-permute-start.23 = (f32[3,2,8,64]{3,2,1,0:T(8,128)S(1)}, f32[3,2,8,64]{3,2,1,0:T(8,128)S(1)}, u32[]{:S(2)}, u32[]{:S(2)}) collective-permute-start(f32[3,2,8,64]{3,2,1,0:T(8,128)S(1)} %fusion.139), channel_id=1, source_target_pairs={{16,0},{32,16},{48,32},{64,48},{80,64},{96,80},{112,96},{128,112},... | collective-permute-start | bytes 36872 | tf_op jit(solution)/shard_map/ppermute | solution.py:19
  217.8 7.0 %collective-permute-start.24 = (f32[3,2,2,2,64]{4,3,2,0,1:T(2,128)S(1)}, f32[3,2,2,2,64]{4,3,2,0,1:T(2,128)S(1)}, u32[]{:S(2)}, u32[]{:S(2)}) collective-permute-start(f32[3,2,2,2,64]{4,3,2,0,1:T(2,128)S(1)} %get-tuple-element.57), channel_id=1, source_target_pairs={{1,0},{2,1},{3,2},{4,3},{5,4},{6,5},{7,6},{8,7},{9,8},{10,9},{11,1... | collective-permute-start | bytes 18440 | tf_op jit(solution)/shard_map/ppermute | solution.py:19
  222.7 5.7 %collective-permute-start.25 = (f32[3,2,2,2,64]{4,3,2,0,1:T(2,128)S(1)}, f32[3,2,2,2,64]{4,3,2,0,1:T(2,128)S(1)}, u32[]{:S(2)}, u32[]{:S(2)}) collective-permute-start(f32[3,2,2,2,64]{4,3,2,0,1:T(2,128)S(1)} %get-tuple-element.56), channel_id=1, source_target_pairs={{0,1},{1,2},{2,3},{3,4},{4,5},{5,6},{6,7},{7,8},{8,9},{9,10},{10,1... | collective-permute-start | bytes 18440 | tf_op jit(solution)/shard_map/ppermute | solution.py:16
  228.4 8.5 %collective-permute-start.26 = (f32[3,2,2,2,64]{4,3,2,0,1:T(2,128)S(1)}, f32[3,2,2,2,64]{4,3,2,0,1:T(2,128)S(1)}, u32[]{:S(2)}, u32[]{:S(2)}) collective-permute-start(f32[3,2,2,2,64]{4,3,2,0,1:T(2,128)S(1)} %get-tuple-element.55), channel_id=1, source_target_pairs={{0,1},{1,2},{2,3},{3,4},{4,5},{5,6},{6,7},{7,8},{8,9},{9,10},{10,1... | collective-permute-start | bytes 18440 | tf_op jit(solution)/shard_map/ppermute | solution.py:16
  230.4 6.5 %collective-permute-start.27 = (f32[3,2,2,2,64]{4,3,2,0,1:T(2,128)S(1)}, f32[3,2,2,2,64]{4,3,2,0,1:T(2,128)S(1)}, u32[]{:S(2)}, u32[]{:S(2)}) collective-permute-start(f32[3,2,2,2,64]{4,3,2,0,1:T(2,128)S(1)} %get-tuple-element.54), channel_id=1, source_target_pairs={{1,0},{2,1},{3,2},{4,3},{5,4},{6,5},{7,6},{8,7},{9,8},{10,9},{11,1... | collective-permute-start | bytes 18440 | tf_op jit(solution)/shard_map/ppermute | solution.py:19
  (2 other events, 7.6 us)
where the time goes:
time: 243 us; the launch traced here: 242 us
  starting transfers between devices  111 us (46%)
  local copies, waits for them, and re-layouts  75.3 us (31%)
  waiting for transfers between devices  45.7 us (19%)
  other arithmetic  8.23 us (3%)
    ppermute x14, starting transfers between devices, padded_2(): lax.ppermute(lax.slice_in_dim(block, block.shape[dim] - width, None, axis...  67.1 us
    ppermute x14, starting transfers between devices, padded_2(): lax.ppermute(lax.slice_in_dim(block, 0, width, axis=dim), axis, backward)  44.1 us
    slice x9, local copies, waits for them, and re-layouts, even_odd(): even_part = lax.slice_in_dim(values, 0, length, stride=2, axis=axis_no)  33.4 us
    slice x6, local copies, waits for them, and re-layouts, even_odd(): odd_part = lax.slice_in_dim(values, 1, length, stride=2, axis=axis_no)  33.4 us
    ppermute x14, waiting for transfers between devices, padded_2(): lax.ppermute(lax.slice_in_dim(block, 0, width, axis=dim), axis, backward)  28.3 us
    ppermute x14, waiting for transfers between devices, padded_2(): lax.ppermute(lax.slice_in_dim(block, block.shape[dim] - width, None, axis...  17.4 us
  transfers between devices with their start and end apart: 28, of which 16 were waited for; matrix products, arithmetic and copies ran while one was open for 3% of the time, Pallas kernels for 0%

commit v1 on v0

v1 whole, which is shorter than its diff:
```python
import functools

import jax
import jax.numpy as jnp
import numpy as np
from jax import lax
from jax.experimental import pallas as pl
from jax.experimental.pallas import tpu as pltpu
from jax.sharding import PartitionSpec as P

F32 = jnp.float32
BF16 = jnp.bfloat16
NX = (16, 8, 4)
NY = (32, 16, 8)
ZH = (2, 1, 1)
REP = (4, 2, 1)
DR = (24, 16, 8)
XK_LOW = (-1, -1, -2)
OWN, XL, XR, YL, YR = range(5)


def z_matrices(count):
    half = count // 2
    even = np.zeros((count, half))
    residual = np.zeros((count, half))
    for k in range(half):
        even[2 * k, k] = 1.0
        residual[2 * k + 1, k] += 1.0
        for at, weight in ((k, -9), (k + 1, -9), (k - 1, 1), (k + 2, 1)):
            residual[2 * (at % half), k] += weight / 16.0
    update = np.zeros((count, half))
    for k in range(half):
        for at, weight in ((k - 1, 9), (k, 9), (k - 2, -1), (k + 1, -1)):
            update[:, k] += weight / 32.0 * residual[:, at % half]
    rows = max(count, 128)
    full = np.zeros((rows, 3, 128))
    for part, matrix in enumerate((even, residual, update)):
        full[:count, part, :half] = matrix
    return full.reshape(rows, 384)


def kernel(
    vel_hbm, flags, table, ix, iy, iz_ref, w1_hbm, w2_hbm, w3_hbm,
    o1_hbm, o2_hbm, o3_hbm, oc_hbm,
    vel, hy, c1, c2, c3, x1, x2, x3, y1, y2, y3, dscr,
    mk, mx1, mx2, mx3, my1, my2, my3, mz1, mz2, mz3, myt, mzt,
    w1, w2, w3, o1, o2, o3, oc,
    send_sem, recv_sem, local_sem,
):
    C, X, Y = (c1, c2, c3), (x1, x2, x3), (y1, y2, y3)
    MX, MY, MZ, W = (mx1, mx2, mx3), (my1, my2, my3), (mz1, mz2, mz3), (w1, w2, w3)
    gx, gy = lax.axis_index("gx"), lax.axis_index("gy")
    nx, ny = lax.axis_size("gx"), lax.axis_size("gy")
    right, left = {"gx": lax.rem(gx + 1, nx)}, {"gx": lax.rem(gx + nx - 1, nx)}
    right2, left2 = {"gx": lax.rem(gx + 2, nx)}, {"gx": lax.rem(gx + nx - 2, nx)}
    up, down = {"gy": lax.rem(gy + 1, ny)}, {"gy": lax.rem(gy + ny - 1, ny)}

    counter = [0]
    pending = []

    def remote(src, dst, device):
        n = counter[0]
        counter[0] += 1
        copy = pltpu.make_async_remote_copy(
            src_ref=src, dst_ref=dst, send_sem=send_sem.at[n], recv_sem=recv_sem.at[n],
            device_id=device, device_id_type=pl.DeviceIdType.MESH,
        )
        copy.start()
        pending.append(copy)
        return copy

    def wait_recv(copies):
        for copy in copies:
            copy.wait_recv()

    local = [
        pltpu.make_async_copy(vel_hbm, vel.at[:, pl.ds(1, 16)], local_sem.at[0]),
        pltpu.make_async_copy(w1_hbm, w1, local_sem.at[1]),
        pltpu.make_async_copy(w2_hbm, w2, local_sem.at[2]),
        pltpu.make_async_copy(w3_hbm, w3, local_sem.at[3]),
    ]
    for copy in local:
        copy.start()

    barrier = pltpu.get_barrier_semaphore()
    for device in (right, left, right2, left2, up, down):
        pl.semaphore_signal(barrier, inc=1, device_id=device, device_id_type=pl.DeviceIdType.MESH)

    for l in range(3):
        for bx in range(2):
            for by in range(4):
                mk[OWN, l, bx, pl.ds(by, 1), :] = jnp.full((1, 128), flags[l, bx, by].astype(F32), F32)
    for j in range(32):
        myt[pl.ds(j, 1), :] = jnp.full((1, 128), table[1, iy[j]], F32)
    iz = iz_ref[...]

    def z_class(c, total):
        return jnp.where(iz == c, table[2, c], total)

    mzt[...] = lax.fori_loop(0, 64, z_class, jnp.zeros((1, 256), F32))

    pl.semaphore_wait(barrier, 6)

    r0 = [
        remote(vel_hbm.at[pl.ds(1, 2), pl.ds(15, 1)], vel.at[pl.ds(1, 2), pl.ds(0, 1)], right),
        remote(vel_hbm.at[pl.ds(1, 2), pl.ds(0, 1)], vel.at[pl.ds(1, 2), pl.ds(17, 1)], left),
    ]
    for at, comp in enumerate((0, 2)):
        r0.append(remote(vel_hbm.at[comp, :, 31], hy.at[0, at], up))
        r0.append(remote(vel_hbm.at[comp, :, 0], hy.at[1, at], down))
    m0 = [
        remote(mk.at[OWN], mk.at[XL], right),
        remote(mk.at[OWN], mk.at[XR], left),
        remote(mk.at[OWN], mk.at[YL], up),
        remote(mk.at[OWN], mk.at[YR], down),
    ]
    local[0].wait()
    wait_recv(r0)

    row = lax.broadcasted_iota(jnp.int32, (32, 256), 0)

    def vorticity(i, carry):
        mx = table[0, ix[i]]
        u, v, w = vel[0, i + 1], vel[1, i + 1], vel[2, i + 1]
        my = jnp.concatenate([myt[...], myt[...]], axis=1)
        mz = mzt[...]

        def along_y(f, at):
            before = jnp.where(row == 0, hy[0, at, pl.ds(i, 1), :], pltpu.roll(f, 1, 0))
            after = jnp.where(row == 31, hy[1, at, pl.ds(i, 1), :], pltpu.roll(f, 31, 0))
            return (after - before) * my

        def along_z(f):
            return (pltpu.roll(f, 255, 1) - pltpu.roll(f, 1, 1)) * mz

        dv_dx = (vel[1, i + 2] - vel[1, i]) * mx
        dw_dx = (vel[2, i + 2] - vel[2, i]) * mx
        curl = (along_y(w, 1) - along_z(v), along_z(u) - dw_dx, dv_dx - along_y(u, 0))
        for c in range(3):
            for h in range(2):
                c1[c, h, i + 6] = curl[c][:, 128 * h : 128 * (h + 1)]
        return carry

    lax.fori_loop(10, 16, vorticity, 0)
    lax.fori_loop(0, 5, vorticity, 0)

    def send_x(l, comps):
        n = NX[l]
        src = lambda start, size: C[l].at[comps, :, pl.ds(start + 6, size)]
        if l < 2:
            return [
                remote(src(n - 6, 1), src(-6, 1), right),
                remote(src(n - 4, 4), src(-4, 4), right),
                remote(src(0, 3), src(n, 3), left),
                remote(src(4, 1), src(n + 4, 1), left),
            ]
        return [
            remote(src(0, 4), src(-4, 4), right),
            remote(src(2, 1), src(-6, 1), right2),
            remote(src(0, 3), src(4, 3), left),
            remote(src(0, 1), src(8, 1), left2),
        ]

    def send_y(l, comps, a):
        n = NY[l]
        part = lambda start: X[l].at[comps, :, a, :, pl.ds(start + 8, 8)]
        return [remote(part(n - 8), part(-8), up), remote(part(0), part(n), down)]

    def lift_x(l, comps):
        half = NX[l] // 2
        tiles = NY[l] // 8

        def body(it, carry):
            h, t = it // tiles, lax.rem(it, tiles)
            rows = pl.ds(pl.multiple_of(t * 8, 8), 8)
            rows_to = pl.ds(pl.multiple_of(t * 8 + 8, 8), 8)
            for c in comps:
                p = lambda i: C[l][c, h, i + 6, rows, :]
                d = {}
                for k in range(-2, half + 1):
                    mask = MX[l][k // REP[l] - XK_LOW[l], rows, :]
                    d[k] = (p(2 * k + 1) - (9.0 * (p(2 * k) + p(2 * k + 2)) - (p(2 * k - 2) + p(2 * k + 4))) * 0.0625) * mask
                for k in range(half):
                    smooth = p(2 * k) + (9.0 * (d[k - 1] + d[k]) - (d[k - 2] + d[k + 1])) * 0.03125
                    X[l][c, h, 0, k, rows_to, :] = smooth
                    X[l][c, h, 1, k, rows_to, :] = d[k]
            return carry

        lax.fori_loop(0, ZH[l] * tiles, body, 0)

    def lift_y(l, c, a):
        half_x, n, r = NX[l] // 2, NY[l] // 2, DR[l]

        def body(h, carry):
            for k in range(half_x):
                line = lambda start, count: X[l][c, h, a, k, pl.ds(start + 8, count, stride=2), :]
                mask = MY[l][k // REP[l]]
                d = (line(-3, r) - (9.0 * (line(-4, r) + line(-2, r)) - (line(-6, r) + line(0, r))) * 0.0625) * mask
                dscr[k, 0:r] = d
                part = lambda s: dscr[k, s : s + n]
                own = part(2)
                smooth = line(0, n) + (9.0 * (part(1) + own) - (part(0) + part(3))) * 0.03125
                at = (c * half_x + k) * n
                Y[l][2 * a, h, at : at + n] = smooth
                Y[l][2 * a + 1, h, at : at + n] = own
            return carry

        lax.fori_loop(0, ZH[l], body, 0)

    def lift_z(l, c, ab):
        half_x, n = NX[l] // 2, NY[l] // 2
        size = half_x * n
        acc = None
        for h in range(ZH[l]):
            x = Y[l][ab, h, c * size : (c + 1) * size, :]
            weights = W[l][h * 128 : (h + 1) * 128, :]
            hi = x.astype(BF16)
            rest = x - hi.astype(F32)
            mid = rest.astype(BF16)
            low = (rest - mid.astype(F32)).astype(BF16)
            for piece in (low, mid, hi):
                term = jnp.dot(piece, weights, preferred_element_type=F32)
                acc = term if acc is None else acc + term
        mask = MZ[l][...]
        smooth = acc[:, :128] + mask * acc[:, 256:]
        detail = mask * acc[:, 128:256]
        lanes = (128, 64, 32)[l]
        out = (o1, o2, o3)[l]
        for k in range(half_x):
            rows = slice(k * n, (k + 1) * n)
            out[c, 2 * ab, k] = detail[rows, :lanes]
            if ab > 0:
                out[c, 2 * ab - 1, k] = smooth[rows, :lanes]
            elif l < 2:
                C[l + 1][c, 0, k + 6] = smooth[rows]
            else:
                oc[c, k] = smooth[rows, :lanes]

    everything = (0, 1, 2)
    all_comps = pl.ds(0, 3)
    x_in = [send_x(0, c) for c in everything]
    lax.fori_loop(5, 10, vorticity, 0)

    wait_recv(m0)
    for l in range(3):
        per = 2 * REP[l]
        for at in range(MX[l].shape[0]):
            bx = at + XK_LOW[l]
            slot = XL if bx < 0 else XR if bx > 1 else OWN
            for by in range(4):
                MX[l][at, pl.ds(by * per, per), :] = jnp.broadcast_to(mk[slot, l, bx % 2, pl.ds(by, 1), :], (per, 128))
        n = NY[l] // 2
        for bx in range(2):
            for m in range(-2, DR[l] - 2):
                by = min(m // REP[l], 4)
                slot = YL if by < 0 else YR if by > 3 else OWN
                MY[l][bx, pl.ds(m + 2, 1), :] = mk[slot, l, bx, pl.ds(by % 4, 1), :]
        for k in range(NX[l] // 2):
            MZ[l][k * n : (k + 1) * n] = MY[l][k // REP[l], 2 : 2 + n]
    for copy in local[1:]:
        copy.wait()

    y_in = []
    for c in everything:
        wait_recv(x_in[c])
        lift_x(0, (c,))
        y_in.append([send_y(0, c, a) for a in range(2)])
    for c in everything:
        wait_recv(y_in[c][0])
        lift_y(0, c, 0)
        lift_z(0, c, 0)
    x_in2 = send_x(1, all_comps)
    for c in everything:
        lift_z(0, c, 1)
    wait_recv(x_in2)
    lift_x(1, everything)
    y_in2 = [send_y(1, all_comps, a) for a in range(2)]
    for c in everything:
        wait_recv(y_in[c][1])
        lift_y(0, c, 1)
    for a in range(2):
        wait_recv(y_in2[a])
    for c in everything:
        lift_y(1, c, 0)
        lift_z(1, c, 0)
    x_in3 = send_x(2, all_comps)
    for c in everything:
        lift_y(1, c, 1)
        for ab in range(1, 4):
            lift_z(1, c, ab)
        lift_z(0, c, 2)
    outs = [pltpu.make_async_copy(o2, o2_hbm, local_sem.at[5])]
    outs[0].start()
    wait_recv(x_in3)
    lift_x(2, everything)
    y_in3 = [send_y(2, all_comps, a) for a in range(2)]
    for c in everything:
        lift_z(0, c, 3)
    outs.append(pltpu.make_async_copy(o1, o1_hbm, local_sem.at[4]))
    outs[1].start()
    for a in range(2):
        wait_recv(y_in3[a])
    for c in everything:
        for a in range(2):
            lift_y(2, c, a)
        for ab in range(4):
            lift_z(2, c, ab)
    outs.append(pltpu.make_async_copy(o3, o3_hbm, local_sem.at[6]))
    outs.append(pltpu.make_async_copy(oc, oc_hbm, local_sem.at[7]))
    for copy in outs[2:]:
        copy.start()
    for copy in pending:
        copy.wait_send()
    for copy in outs:
        copy.wait()


def on_device(velocity, refine_flags, metric_table, index_x, index_y, index_z):
    weights = [jnp.asarray(z_matrices(count).astype(np.float32)).astype(BF16) for count in (256, 128, 64)]
    anywhere = pl.BlockSpec(memory_space=pl.ANY)
    smem = pl.BlockSpec(memory_space=pltpu.SMEM)
    vmem = pl.BlockSpec(memory_space=pltpu.VMEM)
    out_shapes = [(3, 7, 8, 16, 128), (3, 7, 4, 8, 64), (3, 7, 2, 4, 32), (3, 2, 4, 32)]
    v = pltpu.VMEM
    scratch = [v((3, 18, 32, 256), F32), v((2, 2, 16, 256), F32)]
    scratch += [v((3, ZH[l], NX[l] + 11, NY[l], 128), F32) for l in range(3)]
    scratch += [v((3, ZH[l], 2, NX[l] // 2, NY[l] + 24, 128), F32) for l in range(3)]
    scratch += [v((4, ZH[l], 3 * NX[l] * NY[l] // 4, 128), F32) for l in range(3)]
    scratch += [v((8, 32, 128), F32), v((5, 3, 2, 8, 128), F32)]
    scratch += [v((4 if l < 2 else 5, NY[l], 128), F32) for l in range(3)]
    scratch += [v((2, DR[l], 128), F32) for l in range(3)]
    scratch += [v((NX[l] * NY[l] // 4, 128), F32) for l in range(3)]
    scratch += [v((32, 128), F32), v((1, 256), F32)]
    scratch += [v((256, 384), BF16), v((128, 384), BF16), v((128, 384), BF16)]
    scratch += [v(shape, F32) for shape in out_shapes]
    scratch += [pltpu.SemaphoreType.DMA((64,)), pltpu.SemaphoreType.DMA((64,)), pltpu.SemaphoreType.DMA((8,))]
    return pl.pallas_call(
        kernel,
        out_shape=[jax.ShapeDtypeStruct(shape, F32) for shape in out_shapes],
        in_specs=[anywhere, smem, smem, smem, smem, vmem, anywhere, anywhere, anywhere],
        out_specs=[anywhere] * 4,
        scratch_shapes=scratch,
        compiler_params=pltpu.CompilerParams(collective_id=0, has_side_effects=True),
        name="analysis",
    )(velocity, refine_flags, metric_table, index_x, index_y, index_z.reshape(1, 256), *weights)


def solution(mesh):
    return jax.shard_map(
        on_device,
        mesh=mesh,
        in_specs=(P(None, "gx", "gy", None), P(None, "gx", "gy"), P(), P("gx"), P("gy"), P()),
        out_specs=(
            P(None, None, "gx", "gy", None),
            P(None, None, "gx", "gy", None),
            P(None, None, "gx", "gy", None),
            P(None, "gx", "gy", None),
        ),
        check_vma=False,
    )
```

time: 243 us -> 59.2 us (0.24)
  the two profiles are of different devices: /device:TPU:31 before, /device:TPU:1 now
where the time goes in v1:
time: 59.2 us; the launch traced here: 59 us
  Pallas kernels  53.8 us (91%)
  local copies, waits for them, and re-layouts  4.58 us (8%)
  between operations  0.67 us (1%)
    pallas_call x1, Pallas kernels, on_device(): pl.pallas_call(kernel, out_shape=[jax.ShapeDtypeStruct(shape, F32) for sh...  53.8 us
    unnamed x10, local copies, waits for them, and re-layouts  4.58 us

profile of v1, /device:TPU:1, one launch (start us, length us, event | category | flops | bytes accessed | tf_op | source)
XLA Modules:
  0.0 59.0 jit_solution(14306727967650637919)
XLA Ops:
  0.6 53.8 %analysis.1 = (f32[3,7,8,16,128]{4,3,2,1,0:T(8,128)}, f32[3,7,4,8,64]{4,3,2,1,0:T(8,128)}, f32[3,7,2,4,32]{4,3,2,1,0:T(4,128)}, f32[3,2,4,32]{3,2,1,0:T(4,128)}) custom-call(f32[3,16,32,256]{3,2,1,0:T(8,128)} %vel_hbm.1, s32[3,2,4]{2,1,0:T(2,128)} %flags.1, f32[3,64]{1,0:T(4,128)} %table.1, s32[16]{0:T(128)} %ix.1, s32[32]{0:T(128)} %iy.1, ...), custom_call_target="tpu_custom_call" | custom-call | tf_op jit(solution)/shard_map/analysis/pallas_call | solution.py:337
  54.4 0.0 copy-start
  54.4 0.0 copy-start.1
  54.4 0.0 copy-start.2
  54.5 2.6 %copy.17 = f32[3,7,8,16,128]{4,3,2,1,0:T(8,128)} copy(f32[3,7,8,16,128]{4,3,2,1,0:T(8,128)} %get-tuple-element.8) | data formatting | bytes 2752512
  57.1 0.0 copy-done
  57.1 0.7 %copy.18 = f32[3,7,4,8,64]{4,3,2,1,0:T(8,128)} copy(f32[3,7,4,8,64]{4,3,2,1,0:T(8,128)S(1)} %copy-done) | data formatting | bytes 344064
  57.8 0.0 copy-done.1
  57.8 0.6 %copy.19 = f32[3,7,2,4,32]{4,3,2,1,0:T(4,128)} copy(f32[3,7,2,4,32]{4,3,2,1,0:T(4,128)S(1)} %copy-done.1) | data formatting | bytes 43008
  58.4 0.0 copy-done.2
  58.4 0.6 %copy.20 = f32[3,2,4,32]{3,2,1,0:T(4,128)} copy(f32[3,2,4,32]{3,2,1,0:T(4,128)S(1)} %copy-done.2) | data formatting | bytes 6144
Async XLA Ops:
  54.4 2.6 %copy-start = (f32[3,7,4,8,64]{4,3,2,1,0:T(8,128)S(1)}, f32[3,7,4,8,64]{4,3,2,1,0:T(8,128)}, u32[]{:S(2)}) copy-start(f32[3,7,4,8,64]{4,3,2,1,0:T(8,128)} %get-tuple-element.9) | copy-start | bytes 516100
  54.4 3.4 %copy-start.1 = (f32[3,7,2,4,32]{4,3,2,1,0:T(4,128)S(1)}, f32[3,7,2,4,32]{4,3,2,1,0:T(4,128)}, u32[]{:S(2)}) copy-start(f32[3,7,2,4,32]{4,3,2,1,0:T(4,128)} %get-tuple-element.10) | copy-start | bytes 64516
  54.4 4.0 %copy-start.2 = (f32[3,2,4,32]{3,2,1,0:T(4,128)S(1)}, f32[3,2,4,32]{3,2,1,0:T(4,128)}, u32[]{:S(2)}) copy-start(f32[3,2,4,32]{3,2,1,0:T(4,128)} %get-tuple-element.11) | copy-start | bytes 9220

commit v2 on v1

v2 whole, which is shorter than its diff:
```python
import functools

import jax
import jax.numpy as jnp
import numpy as np
from jax import lax
from jax.experimental import pallas as pl
from jax.experimental.pallas import tpu as pltpu
from jax.sharding import PartitionSpec as P

F32 = jnp.float32
BF16 = jnp.bfloat16
NX = (16, 8, 4)
NY = (32, 16, 8)
ZH = (2, 1, 1)
REP = (4, 2, 1)
DR = (24, 16, 8)
XK_LOW = (-1, -1, -2)
ROWS = (0, 8, 8)


def slot(sx, sy):
    return 3 * (sx + 1) + sy + 1


def z_matrices(count):
    half = count // 2
    even = np.zeros((count, half))
    residual = np.zeros((count, half))
    for k in range(half):
        even[2 * k, k] = 1.0
        residual[2 * k + 1, k] += 1.0
        for at, weight in ((k, -9), (k + 1, -9), (k - 1, 1), (k + 2, 1)):
            residual[2 * (at % half), k] += weight / 16.0
    update = np.zeros((count, half))
    for k in range(half):
        for at, weight in ((k - 1, 9), (k, 9), (k - 2, -1), (k + 1, -1)):
            update[:, k] += weight / 32.0 * residual[:, at % half]
    rows = max(count, 128)
    full = np.zeros((rows, 3, 128))
    for part, matrix in enumerate((even, residual, update)):
        full[:count, part, :half] = matrix
    return full.reshape(rows, 384)


def kernel(
    vel_hbm, flags, table, ix, iy, iz_ref, w1_hbm, w2_hbm, w3_hbm,
    o1, o2, o3, oc,
    vel, hy, c1, c2, c3, x1, x2, x3, y1, y2, y3, dscr,
    mk, mx1, mx2, mx3, my1, my2, my3, mz1, mz2, mz3, mxt, myt, mzt,
    w1, w2, w3,
    send_sem, recv_sem, local_sem,
):
    C, X, Y = (c1, c2, c3), (x1, x2, x3), (y1, y2, y3)
    MX, MY, MZ, W = (mx1, mx2, mx3), (my1, my2, my3), (mz1, mz2, mz3), (w1, w2, w3)
    gx, gy = lax.axis_index("gx"), lax.axis_index("gy")
    nx, ny = lax.axis_size("gx"), lax.axis_size("gy")

    def at(dx, dy):
        return {"gx": lax.rem(gx + (nx + dx), nx), "gy": lax.rem(gy + (ny + dy), ny)}

    counter = [0]
    pending = []

    def remote(src, dst, device):
        n = counter[0]
        counter[0] += 1
        copy = pltpu.make_async_remote_copy(
            src_ref=src, dst_ref=dst, send_sem=send_sem.at[n], recv_sem=recv_sem.at[n],
            device_id=device, device_id_type=pl.DeviceIdType.MESH,
        )
        copy.start()
        pending.append(copy)
        return copy

    def wait_recv(copies):
        for copy in copies:
            copy.wait_recv()

    local = [
        pltpu.make_async_copy(vel_hbm, vel.at[:, pl.ds(7, 16)], local_sem.at[0]),
        pltpu.make_async_copy(w1_hbm, w1, local_sem.at[1]),
        pltpu.make_async_copy(w2_hbm, w2, local_sem.at[2]),
        pltpu.make_async_copy(w3_hbm, w3, local_sem.at[3]),
    ]
    for copy in local:
        copy.start()

    around = [(dx, dy) for dx in (-2, -1, 0, 1, 2) for dy in (-1, 0, 1) if (dx, dy) != (0, 0)]
    barrier = pltpu.get_barrier_semaphore()
    for step in around:
        pl.semaphore_signal(barrier, inc=1, device_id=at(*step), device_id_type=pl.DeviceIdType.MESH)

    own = slot(0, 0)
    for l in range(3):
        for bx in range(2):
            for by in range(4):
                mk[own, l, bx, pl.ds(by, 1), :] = jnp.full((1, 128), flags[l, bx, by].astype(F32), F32)
    for i in range(16):
        mxt[pl.ds(i + 6, 1), :] = jnp.full((1, 128), table[0, ix[i]], F32)
    for j in range(32):
        myt[pl.ds(j, 1), :] = jnp.full((1, 128), table[1, iy[j]], F32)
    iz = iz_ref[...]

    def z_class(c, total):
        return jnp.where(iz == c, table[2, c], total)

    mzt[...] = lax.fori_loop(0, 64, z_class, jnp.zeros((1, 256), F32))

    pl.semaphore_wait(barrier, len(around))

    def send_rows(dx, dy, place, line):
        start, size, to = ((0, 8, 24), (0, 16, 8), (8, 8, 0))[dx + 1]
        return remote(vel_hbm.at[:, pl.ds(start, size), line], hy.at[place, :, pl.ds(to, size)], at(dx, dy))

    corner_rows = [send_rows(dx, dy, place, line) for dx in (1, -1) for dy, place, line in ((1, 0, 31), (-1, 1, 0))]
    own_rows = [send_rows(0, 1, 0, 31), send_rows(0, -1, 1, 0)]
    inner_rows = [send_rows(dx, 0, place, line) for dx in (1, -1) for place, line in ((2, 8), (3, 23))]
    metric_in = [
        remote(mxt.at[pl.ds(16, 6)], mxt.at[pl.ds(0, 6)], at(1, 0)),
        remote(mxt.at[pl.ds(6, 5)], mxt.at[pl.ds(22, 5)], at(-1, 0)),
    ]
    flags_in = [remote(mk.at[own], mk.at[slot(-dx, -dy)], at(dx, dy)) for dx, dy in around if abs(dx) < 2]

    def send_planes(first, size):
        rows = pl.ds(first, size)
        copies = []
        for dx, start, to, count in ((1, 9, -7, 7), (-1, 0, 16, 6)):
            skip = 1 if dx > 0 else 0
            copies.append(remote(
                vel_hbm.at[pl.ds(1, 2), pl.ds(start, count), rows], vel.at[pl.ds(1, 2), pl.ds(to + 7, count), rows], at(dx, 0)))
            copies.append(remote(
                vel_hbm.at[0, pl.ds(start + skip, count - 1), rows], vel.at[0, pl.ds(to + skip + 7, count - 1), rows], at(dx, 0)))
        return copies

    outer = send_planes(0, 8) + send_planes(24, 8)
    inner = send_planes(8, 16)

    row = lax.broadcasted_iota(jnp.int32, (8, 256), 0)

    def vorticity(lo, hi, tiles, halo):
        def body(i, carry):
            mx = jnp.concatenate([mxt[pl.ds(i + 6, 1), :]] * 2, axis=1)
            mz = mzt[...]
            for t in tiles:
                rows = slice(8 * t, 8 * t + 8)
                u, v, w = vel[0, i + 7, rows], vel[1, i + 7, rows], vel[2, i + 7, rows]
                my = jnp.concatenate([myt[rows, :]] * 2, axis=1)

                def along_y(f, c):
                    place = 0 if t == 0 else 3 if halo and t == 3 else None
                    first = vel[c, i + 7, 8 * t - 1 : 8 * t] if place is None else hy[place, c, pl.ds(i + 8, 1), :]
                    place = 1 if t == 3 else 2 if halo and t == 0 else None
                    last = vel[c, i + 7, 8 * t + 8 : 8 * t + 9] if place is None else hy[place, c, pl.ds(i + 8, 1), :]
                    before = jnp.where(row == 0, first, pltpu.roll(f, 1, 0))
                    after = jnp.where(row == 7, last, pltpu.roll(f, 7, 0))
                    return (after - before) * my

                def along_z(f):
                    return (pltpu.roll(f, 255, 1) - pltpu.roll(f, 1, 1)) * mz

                dv_dx = (vel[1, i + 8, rows] - vel[1, i + 6, rows]) * mx
                dw_dx = (vel[2, i + 8, rows] - vel[2, i + 6, rows]) * mx
                curl = (along_y(w, 2) - along_z(v), along_z(u) - dw_dx, dv_dx - along_y(u, 0))
                for c in range(3):
                    for h in range(2):
                        c1[c, h, i + 6, rows] = curl[c][:, 128 * h : 128 * (h + 1)]
            return carry

        lax.fori_loop(lo, hi, body, 0)

    def lift_x(l, comps, tiles):
        half = NX[l] // 2
        first, step, count = tiles

        def body(it, carry):
            h, t = it // count, first + step * lax.rem(it, count)
            rows = pl.ds(pl.multiple_of(t * 8, 8), 8)
            rows_to = pl.ds(pl.multiple_of(t * 8 + 8 - ROWS[l], 8), 8)
            for c in comps:
                p = lambda i: C[l][c, h, i + 6, rows, :]
                d = {}
                for k in range(-2, half + 1):
                    mask = MX[l][k // REP[l] - XK_LOW[l], rows, :]
                    d[k] = (p(2 * k + 1) - (9.0 * (p(2 * k) + p(2 * k + 2)) - (p(2 * k - 2) + p(2 * k + 4))) * 0.0625) * mask
                for k in range(half):
                    smooth = p(2 * k) + (9.0 * (d[k - 1] + d[k]) - (d[k - 2] + d[k + 1])) * 0.03125
                    X[l][c, h, 0, k, rows_to, :] = smooth
                    X[l][c, h, 1, k, rows_to, :] = d[k]
            return carry

        lax.fori_loop(0, ZH[l] * count, body, 0)

    def lift_y(l, c, a):
        half_x, n, r = NX[l] // 2, NY[l] // 2, DR[l]

        def body(h, carry):
            for k in range(half_x):
                line = lambda start, count: X[l][c, h, a, k, pl.ds(start + 8, count, stride=2), :]
                mask = MY[l][k // REP[l]]
                d = (line(-3, r) - (9.0 * (line(-4, r) + line(-2, r)) - (line(-6, r) + line(0, r))) * 0.0625) * mask
                dscr[k, 0:r] = d
                part = lambda s: dscr[k, s : s + n]
                own_part = part(2)
                smooth = line(0, n) + (9.0 * (part(1) + own_part) - (part(0) + part(3))) * 0.03125
                to = (c * half_x + k) * n
                Y[l][2 * a, h, to : to + n] = smooth
                Y[l][2 * a + 1, h, to : to + n] = own_part
            return carry

        lax.fori_loop(0, ZH[l], body, 0)

    def lift_z(l, ab):
        half_x, n = NX[l] // 2, NY[l] // 2
        acc = None
        for h in range(ZH[l]):
            x = Y[l][ab, h]
            weights = W[l][h * 128 : (h + 1) * 128, :]
            hi = x.astype(BF16)
            rest = x - hi.astype(F32)
            mid = rest.astype(BF16)
            low = (rest - mid.astype(F32)).astype(BF16)
            for piece in (low, mid, hi):
                term = jnp.dot(piece, weights, preferred_element_type=F32)
                acc = term if acc is None else acc + term
        mask = jnp.concatenate([MZ[l][...]] * 3, axis=0)
        smooth = acc[:, :128] + mask * acc[:, 256:]
        detail = mask * acc[:, 128:256]
        lanes = (128, 64, 32)[l]
        out = (o1, o2, o3)[l]
        for c in range(3):
            for k in range(half_x):
                rows = slice((c * half_x + k) * n, (c * half_x + k + 1) * n)
                out[c, 2 * ab, k] = detail[rows, :lanes]
                if ab > 0:
                    out[c, 2 * ab - 1, k] = smooth[rows, :lanes]
                elif l < 2:
                    C[l + 1][c, 0, k + 6, 8 : 8 + n] = smooth[rows]
                else:
                    oc[c, k] = smooth[rows, :lanes]

    def send_lines(c, a):
        return [
            remote(x1.at[c, :, a, :, pl.ds(34, 6)], x1.at[c, :, a, :, pl.ds(2, 6)], at(0, 1)),
            remote(x1.at[c, :, a, :, pl.ds(8, 5)], x1.at[c, :, a, :, pl.ds(40, 5)], at(0, -1)),
        ]

    def send_around(l):
        n, m = NX[l], NY[l]
        if l == 1:
            planes = ((1, n - 6, 1), (1, n - 4, 4), (-1, 0, 3), (-1, 4, 1))
        else:
            planes = ((1, 0, 4), (2, 2, 1), (-1, 0, 3), (-2, 0, 1))
        rows = ((1, m - 6, 6), (-1, 0, 5))
        moves = [(dx, dy, i, ci, j, cj) for dx, i, ci in planes for dy, j, cj in rows]
        moves += [(dx, 0, i, ci, 0, m) for dx, i, ci in planes]
        moves += [(0, dy, 0, n, j, cj) for dy, j, cj in rows]
        copies = []
        for dx, dy, i, ci, j, cj in moves:
            src = C[l].at[:, 0, pl.ds(i + 6, ci), pl.ds(j + 8, cj)]
            dst = C[l].at[:, 0, pl.ds(i + 6 - dx * n, ci), pl.ds(j + 8 - dy * m, cj)]
            copies.append(remote(src, dst, at(dx, dy)))
        return copies

    everything = (0, 1, 2)
    local[0].wait()
    wait_recv(own_rows)
    vorticity(1, 15, (0, 1, 2, 3), False)

    wait_recv(metric_in + flags_in)
    for l in range(3):
        per = 2 * REP[l]
        low = -ROWS[l] // per
        for k in range(MX[l].shape[0]):
            bx = k + XK_LOW[l]
            for by in range(low, NY[l] // per - low):
                place = slot(-1 if bx < 0 else 1 if bx > 1 else 0, -1 if by < 0 else 1 if by > 3 else 0)
                value = jnp.broadcast_to(mk[place, l, bx % 2, pl.ds(by % 4, 1), :], (per, 128))
                MX[l][k, pl.ds((by - low) * per, per), :] = value
        n = NY[l] // 2
        for bx in range(2):
            for m in range(-2, DR[l] - 2):
                by = min(m // REP[l], 4)
                place = slot(0, -1 if by < 0 else 1 if by > 3 else 0)
                MY[l][bx, pl.ds(m + 2, 1), :] = mk[place, l, bx, pl.ds(by % 4, 1), :]
        for k in range(NX[l] // 2):
            MZ[l][k * n : (k + 1) * n] = MY[l][k // REP[l], 2 : 2 + n]
    for copy in local[1:]:
        copy.wait()

    wait_recv(corner_rows + inner_rows + outer)
    vorticity(-6, 0, (0, 3), True)
    vorticity(0, 1, (0, 3), False)
    vorticity(15, 16, (0, 3), False)
    vorticity(16, 21, (0, 3), True)
    lines = []
    for c in everything:
        lift_x(0, (c,), (0, 3, 2))
        lines.append(send_lines(c, 0))
    wait_recv(inner)
    vorticity(-6, 0, (1, 2), True)
    vorticity(0, 1, (1, 2), False)
    vorticity(15, 16, (1, 2), False)
    vorticity(16, 21, (1, 2), True)
    for c in everything:
        lift_x(0, (c,), (1, 1, 2))
    for c in everything:
        wait_recv(lines[c])
        lift_y(0, c, 0)
    lift_z(0, 0)
    around2 = send_around(1)
    lines = [send_lines(c, 1) for c in everything]
    lift_z(0, 1)
    wait_recv(around2)
    lift_x(1, everything, (0, 1, 4))
    for c in everything:
        lift_y(1, c, 0)
    lift_z(1, 0)
    around3 = send_around(2)
    for c in everything:
        lift_y(1, c, 1)
    for ab in range(1, 4):
        lift_z(1, ab)
    for c in everything:
        wait_recv(lines[c])
        lift_y(0, c, 1)
    lift_z(0, 2)
    lift_z(0, 3)
    wait_recv(around3)
    lift_x(2, everything, (0, 1, 3))
    for c in everything:
        for a in range(2):
            lift_y(2, c, a)
    for ab in range(4):
        lift_z(2, ab)
    for copy in pending:
        copy.wait_send()


def write_out(*refs):
    sem = refs[8]
    copies = [pltpu.make_async_copy(refs[n], refs[4 + n], sem.at[n]) for n in range(4)]
    for copy in copies:
        copy.start()
    for copy in copies:
        copy.wait()


def on_device(velocity, refine_flags, metric_table, index_x, index_y, index_z):
    weights = [jnp.asarray(z_matrices(count).astype(np.float32)).astype(BF16) for count in (256, 128, 64)]
    anywhere = pl.BlockSpec(memory_space=pl.ANY)
    smem = pl.BlockSpec(memory_space=pltpu.SMEM)
    vmem = pl.BlockSpec(memory_space=pltpu.VMEM)
    out_shapes = [(3, 7, 8, 16, 128), (3, 7, 4, 8, 64), (3, 7, 2, 4, 32), (3, 2, 4, 32)]
    v = pltpu.VMEM
    scratch = [v((3, 29, 32, 256), F32), v((4, 3, 32, 256), F32)]
    scratch += [v((3, ZH[l], NX[l] + 11, NY[l] + 2 * ROWS[l], 128), F32) for l in range(3)]
    scratch += [v((3, ZH[l], 2, NX[l] // 2, NY[l] + 24, 128), F32) for l in range(3)]
    scratch += [v((4, ZH[l], 3 * NX[l] * NY[l] // 4, 128), F32) for l in range(3)]
    scratch += [v((8, 32, 128), F32), v((9, 3, 2, 4, 128), F32)]
    scratch += [v((4 if l < 2 else 5, NY[l] + 2 * ROWS[l], 128), F32) for l in range(3)]
    scratch += [v((2, DR[l], 128), F32) for l in range(3)]
    scratch += [v((NX[l] * NY[l] // 4, 128), F32) for l in range(3)]
    scratch += [v((32, 128), F32), v((32, 128), F32), v((1, 256), F32)]
    scratch += [v((256, 384), BF16), v((128, 384), BF16), v((128, 384), BF16)]
    scratch += [pltpu.SemaphoreType.DMA((96,)), pltpu.SemaphoreType.DMA((96,)), pltpu.SemaphoreType.DMA((8,))]
    results = pl.pallas_call(
        kernel,
        out_shape=[v(shape, F32) for shape in out_shapes],
        in_specs=[anywhere, smem, smem, smem, smem, vmem, anywhere, anywhere, anywhere],
        out_specs=[vmem] * 4,
        scratch_shapes=scratch,
        compiler_params=pltpu.CompilerParams(collective_id=0, has_side_effects=True),
        name="analysis",
    )(velocity, refine_flags, metric_table, index_x, index_y, index_z.reshape(1, 256), *weights)
    return pl.pallas_call(
        write_out,
        out_shape=[jax.ShapeDtypeStruct(shape, F32) for shape in out_shapes],
        in_specs=[vmem] * 4,
        out_specs=[anywhere] * 4,
        scratch_shapes=[pltpu.SemaphoreType.DMA((4,))],
        name="write_out",
    )(*[pltpu.with_memory_space_constraint(result, pltpu.VMEM) for result in results])


def solution(mesh):
    return jax.shard_map(
        on_device,
        mesh=mesh,
        in_specs=(P(None, "gx", "gy", None), P(None, "gx", "gy"), P(), P("gx"), P("gy"), P()),
        out_specs=(
            P(None, None, "gx", "gy", None),
            P(None, None, "gx", "gy", None),
            P(None, None, "gx", "gy", None),
            P(None, "gx", "gy", None),
        ),
        check_vma=False,
    )
```

time: 59.2 us -> 46.5 us (0.79)
  Pallas kernels: 53.8 us -> 45.8 us
  local copies, waits for them, and re-layouts: 4.58 us -> 0 us
    pallas_call x1 -> x2, Pallas kernels: 53.8 us -> 45.8 us  [the longest x1 44.5 us: on_device(): pl.pallas_call(kernel, out_shape=[v(shape, F32) for shape in out_shapes],...]
    unnamed x10 -> x0, local copies, waits for them, and re-layouts: 4.58 us -> none
where the time goes in v2:
time: 46.5 us; the launch traced here: 46.4 us
  Pallas kernels  45.8 us (98%)
  between operations  0.64 us (1%)
    pallas_call x1, Pallas kernels, on_device(): pl.pallas_call(kernel, out_shape=[v(shape, F32) for shape in out_shapes],...  44.5 us
    pallas_call x1, Pallas kernels, on_device(): pl.pallas_call(write_out, out_shape=[jax.ShapeDtypeStruct(shape, F32) for...  1.24 us

profile of v2, /device:TPU:1, one launch (start us, length us, event | category | flops | bytes accessed | tf_op | source)
XLA Modules:
  0.0 46.4 jit_solution(11531040945163245918)
XLA Ops:
  0.6 44.5 %analysis.1 = (f32[3,7,8,16,128]{4,3,2,1,0:T(8,128)S(1)}, f32[3,7,4,8,64]{4,3,2,1,0:T(8,128)S(1)}, f32[3,7,2,4,32]{4,3,2,1,0:T(4,128)S(1)}, f32[3,2,4,32]{3,2,1,0:T(4,128)S(1)}) custom-call(f32[3,16,32,256]{3,2,1,0:T(8,128)} %vel_hbm.1, s32[3,2,4]{2,1,0:T(2,128)} %flags.1, f32[3,64]{1,0:T(4,128)} %table.1, s32[16]{0:T(128)} %ix.1, s32[32]{0:T(128)} %iy.1, ...), custom_call_target="tpu_custom_call" | custom-call | tf_op jit(solution)/shard_map/analysis/pallas_call | solution.py:367
  45.2 1.2 %write_out.1 = (f32[3,7,8,16,128]{4,3,2,1,0:T(8,128)}, f32[3,7,4,8,64]{4,3,2,1,0:T(8,128)}, f32[3,7,2,4,32]{4,3,2,1,0:T(4,128)}, f32[3,2,4,32]{3,2,1,0:T(4,128)}) custom-call(f32[3,7,8,16,128]{4,3,2,1,0:T(8,128)S(1)} %get-tuple-element.8.refs_0_, f32[3,7,4,8,64]{4,3,2,1,0:T(8,128)S(1)} %get-tuple-element.9.refs_1_, ...), custom_call_target="tpu_custom_call" | custom-call | tf_op jit(solution)/shard_map/write_out/pallas_call | solution.py:376

commit v3 on v2

--- a/solution.py
+++ b/solution.py
@@ -86,9 +86,10 @@
     for copy in local:
         copy.start()
 
-    around = [(dx, dy) for dx in (-2, -1, 0, 1, 2) for dy in (-1, 0, 1) if (dx, dy) != (0, 0)]
+    direct = ((1, 0), (-1, 0), (0, 1), (0, -1))
+    diagonal = ((1, 1), (1, -1), (-1, 1), (-1, -1))
     barrier = pltpu.get_barrier_semaphore()
-    for step in around:
+    for step in direct:
         pl.semaphore_signal(barrier, inc=1, device_id=at(*step), device_id_type=pl.DeviceIdType.MESH)
 
     own = slot(0, 0)
@@ -98,29 +99,24 @@
                 mk[own, l, bx, pl.ds(by, 1), :] = jnp.full((1, 128), flags[l, bx, by].astype(F32), F32)
     for i in range(16):
         mxt[pl.ds(i + 6, 1), :] = jnp.full((1, 128), table[0, ix[i]], F32)
-    for j in range(32):
-        myt[pl.ds(j, 1), :] = jnp.full((1, 128), table[1, iy[j]], F32)
-    iz = iz_ref[...]
-
-    def z_class(c, total):
-        return jnp.where(iz == c, table[2, c], total)
-
-    mzt[...] = lax.fori_loop(0, 64, z_class, jnp.zeros((1, 256), F32))
-
-    pl.semaphore_wait(barrier, len(around))
+
+    pl.semaphore_wait(barrier, len(direct))
 
     def send_rows(dx, dy, place, line):
         start, size, to = ((0, 8, 24), (0, 16, 8), (8, 8, 0))[dx + 1]
         return remote(vel_hbm.at[:, pl.ds(start, size), line], hy.at[place, :, pl.ds(to, size)], at(dx, dy))
 
-    corner_rows = [send_rows(dx, dy, place, line) for dx in (1, -1) for dy, place, line in ((1, 0, 31), (-1, 1, 0))]
     own_rows = [send_rows(0, 1, 0, 31), send_rows(0, -1, 1, 0)]
-    inner_rows = [send_rows(dx, 0, place, line) for dx in (1, -1) for place, line in ((2, 8), (3, 23))]
+    inner_rows = [[send_rows(dx, 0, place, line) for dx in (1, -1)] for place, line in ((3, 23), (2, 8))]
     metric_in = [
         remote(mxt.at[pl.ds(16, 6)], mxt.at[pl.ds(0, 6)], at(1, 0)),
         remote(mxt.at[pl.ds(6, 5)], mxt.at[pl.ds(22, 5)], at(-1, 0)),
     ]
-    flags_in = [remote(mk.at[own], mk.at[slot(-dx, -dy)], at(dx, dy)) for dx, dy in around if abs(dx) < 2]
+
+    def send_flags(steps):
+        return [remote(mk.at[own], mk.at[slot(-dx, -dy)], at(dx, dy)) for dx, dy in steps]
+
+    flags_in = send_flags(direct)
 
     def send_planes(first, size):
         rows = pl.ds(first, size)
@@ -133,8 +129,16 @@
                 vel_hbm.at[0, pl.ds(start + skip, count - 1), rows], vel.at[0, pl.ds(to + skip + 7, count - 1), rows], at(dx, 0)))
         return copies
 
-    outer = send_planes(0, 8) + send_planes(24, 8)
-    inner = send_planes(8, 16)
+    outer = [send_planes(24, 8), send_planes(0, 8)]
+    for j in range(32):
+        myt[pl.ds(j, 1), :] = jnp.full((1, 128), table[1, iy[j]], F32)
+    iz = iz_ref[...]
+
+    def z_class(c, total):
+        return jnp.where(iz == c, table[2, c], total)
+
+    mzt[...] = lax.fori_loop(0, 64, z_class, jnp.zeros((1, 256), F32))
+
 
     row = lax.broadcasted_iota(jnp.int32, (8, 256), 0)
 
@@ -239,11 +243,10 @@
                 else:
                     oc[c, k] = smooth[rows, :lanes]
 
-    def send_lines(c, a):
-        return [
-            remote(x1.at[c, :, a, :, pl.ds(34, 6)], x1.at[c, :, a, :, pl.ds(2, 6)], at(0, 1)),
-            remote(x1.at[c, :, a, :, pl.ds(8, 5)], x1.at[c, :, a, :, pl.ds(40, 5)], at(0, -1)),
-        ]
+    def send_lines(c, a, forward):
+        if forward:
+            return remote(x1.at[c, :, a, :, pl.ds(34, 6)], x1.at[c, :, a, :, pl.ds(2, 6)], at(0, 1))
+        return remote(x1.at[c, :, a, :, pl.ds(8, 5)], x1.at[c, :, a, :, pl.ds(40, 5)], at(0, -1))
 
     def send_around(l):
         n, m = NX[l], NY[l]
@@ -263,12 +266,19 @@
         return copies
 
     everything = (0, 1, 2)
+    corner_rows = []
+    for place, copy in ((1, own_rows[1]), (0, own_rows[0])):
+        copy.wait_recv()
+        line = hy.at[place]
+        corner_rows.append([
+            remote(line.at[:, pl.ds(16, 8)], line.at[:, pl.ds(0, 8)], at(1, 0)),
+            remote(line.at[:, pl.ds(8, 8)], line.at[:, pl.ds(24, 8)], at(-1, 0)),
+        ])
+    inner = send_planes(8, 16)
     local[0].wait()
-    wait_recv(own_rows)
-    vorticity(1, 15, (0, 1, 2, 3), False)
-
-    wait_recv(metric_in + flags_in)
-    for l in range(3):
+    vorticity(1, 15, (3, 0, 1, 2), False)
+
+    def masks(l):
         per = 2 * REP[l]
         low = -ROWS[l] // per
         for k in range(MX[l].shape[0]):
@@ -285,18 +295,23 @@
                 MY[l][bx, pl.ds(m + 2, 1), :] = mk[place, l, bx, pl.ds(by % 4, 1), :]
         for k in range(NX[l] // 2):
             MZ[l][k * n : (k + 1) * n] = MY[l][k // REP[l], 2 : 2 + n]
+
+    wait_recv(metric_in + flags_in)
+    masks(0)
     for copy in local[1:]:
         copy.wait()
 
-    wait_recv(corner_rows + inner_rows + outer)
-    vorticity(-6, 0, (0, 3), True)
-    vorticity(0, 1, (0, 3), False)
-    vorticity(15, 16, (0, 3), False)
-    vorticity(16, 21, (0, 3), True)
-    lines = []
-    for c in everything:
-        lift_x(0, (c,), (0, 3, 2))
-        lines.append(send_lines(c, 0))
+    lines = [[], [], []]
+    for n, t in enumerate((3, 0)):
+        wait_recv(corner_rows[n] + inner_rows[n] + outer[n])
+        vorticity(-6, 0, (t,), True)
+        vorticity(0, 1, (t,), False)
+        vorticity(15, 16, (t,), False)
+        vorticity(16, 21, (t,), True)
+        for c in everything:
+            lift_x(0, (c,), (t, 0, 1))
+            lines[c].append(send_lines(c, 0, t == 3))
+    flags_in = send_flags(diagonal)
     wait_recv(inner)
     vorticity(-6, 0, (1, 2), True)
     vorticity(0, 1, (1, 2), False)
@@ -309,7 +324,10 @@
         lift_y(0, c, 0)
     lift_z(0, 0)
     around2 = send_around(1)
-    lines = [send_lines(c, 1) for c in everything]
+    lines = [[send_lines(c, 1, forward) for forward in (True, False)] for c in everything]
+    wait_recv(flags_in)
+    masks(1)
+    masks(2)
     lift_z(0, 1)
     wait_recv(around2)
     lift_x(1, everything, (0, 1, 4))

time: 46.5 us -> 46.4 us (level)
  no operation moved by 1% of the time
where the time goes in v3:
time: 46.4 us; the launch traced here: 46.2 us
  Pallas kernels  45.6 us (98%)
  between operations  0.64 us (1%)
    pallas_call x1, Pallas kernels, on_device(): pl.pallas_call(kernel, out_shape=[v(shape, F32) for shape in out_shapes],...  44.3 us
    pallas_call x1, Pallas kernels, on_device(): pl.pallas_call(write_out, out_shape=[jax.ShapeDtypeStruct(shape, F32) for...  1.24 us

profile of v3, /device:TPU:1, one launch (start us, length us, event | category | flops | bytes accessed | tf_op | source)
XLA Modules:
  0.0 46.2 jit_solution(6828940182321937163)
XLA Ops:
  0.6 44.3 %analysis.1 = (f32[3,7,8,16,128]{4,3,2,1,0:T(8,128)S(1)}, f32[3,7,4,8,64]{4,3,2,1,0:T(8,128)S(1)}, f32[3,7,2,4,32]{4,3,2,1,0:T(4,128)S(1)}, f32[3,2,4,32]{3,2,1,0:T(4,128)S(1)}) custom-call(f32[3,16,32,256]{3,2,1,0:T(8,128)} %vel_hbm.1, s32[3,2,4]{2,1,0:T(2,128)} %flags.1, f32[3,64]{1,0:T(4,128)} %table.1, s32[16]{0:T(128)} %ix.1, s32[32]{0:T(128)} %iy.1, ...), custom_call_target="tpu_custom_call" | custom-call | tf_op jit(solution)/shard_map/analysis/pallas_call | solution.py:385
  45.0 1.2 %write_out.1 = (f32[3,7,8,16,128]{4,3,2,1,0:T(8,128)}, f32[3,7,4,8,64]{4,3,2,1,0:T(8,128)}, f32[3,7,2,4,32]{4,3,2,1,0:T(4,128)}, f32[3,2,4,32]{3,2,1,0:T(4,128)}) custom-call(f32[3,7,8,16,128]{4,3,2,1,0:T(8,128)S(1)} %get-tuple-element.8.refs_0_, f32[3,7,4,8,64]{4,3,2,1,0:T(8,128)S(1)} %get-tuple-element.9.refs_1_, ...), custom_call_target="tpu_custom_call" | custom-call | tf_op jit(solution)/shard_map/write_out/pallas_call | solution.py:394

commit v4 on v3

--- a/solution.py
+++ b/solution.py
@@ -77,6 +77,12 @@
         for copy in copies:
             copy.wait_recv()
 
+    direct = ((1, 0), (-1, 0), (0, 1), (0, -1))
+    diagonal = ((1, 1), (1, -1), (-1, 1), (-1, -1))
+    barrier = pltpu.get_barrier_semaphore()
+    for step in direct:
+        pl.semaphore_signal(barrier, inc=1, device_id=at(*step), device_id_type=pl.DeviceIdType.MESH)
+
     local = [
         pltpu.make_async_copy(vel_hbm, vel.at[:, pl.ds(7, 16)], local_sem.at[0]),
         pltpu.make_async_copy(w1_hbm, w1, local_sem.at[1]),
@@ -85,12 +91,6 @@
     ]
     for copy in local:
         copy.start()
-
-    direct = ((1, 0), (-1, 0), (0, 1), (0, -1))
-    diagonal = ((1, 1), (1, -1), (-1, 1), (-1, -1))
-    barrier = pltpu.get_barrier_semaphore()
-    for step in direct:
-        pl.semaphore_signal(barrier, inc=1, device_id=at(*step), device_id_type=pl.DeviceIdType.MESH)
 
     own = slot(0, 0)
     for l in range(3):
@@ -171,16 +171,21 @@
                         c1[c, h, i + 6, rows] = curl[c][:, 128 * h : 128 * (h + 1)]
             return carry
 
-        lax.fori_loop(lo, hi, body, 0)
+        if len(tiles) < 4:
+            for i in range(lo, hi):
+                body(i, 0)
+        else:
+            lax.fori_loop(lo, hi, body, 0)
 
     def lift_x(l, comps, tiles):
         half = NX[l] // 2
         first, step, count = tiles
 
         def body(it, carry):
-            h, t = it // count, first + step * lax.rem(it, count)
-            rows = pl.ds(pl.multiple_of(t * 8, 8), 8)
-            rows_to = pl.ds(pl.multiple_of(t * 8 + 8 - ROWS[l], 8), 8)
+            h, t = it // count, first + step * (it % count)
+            rows = pl.ds(t * 8 if isinstance(t, int) else pl.multiple_of(t * 8, 8), 8)
+            to = t * 8 + 8 - ROWS[l]
+            rows_to = pl.ds(to if isinstance(t, int) else pl.multiple_of(to, 8), 8)
             for c in comps:
                 p = lambda i: C[l][c, h, i + 6, rows, :]
                 d = {}
@@ -193,7 +198,11 @@
                     X[l][c, h, 1, k, rows_to, :] = d[k]
             return carry
 
-        lax.fori_loop(0, ZH[l] * count, body, 0)
+        if l > 0 or count == 1:
+            for it in range(ZH[l] * count):
+                body(it, 0)
+        else:
+            lax.fori_loop(0, ZH[l] * count, body, 0)
 
     def lift_y(l, c, a):
         half_x, n, r = NX[l] // 2, NY[l] // 2, DR[l]
@@ -203,8 +212,9 @@
                 line = lambda start, count: X[l][c, h, a, k, pl.ds(start + 8, count, stride=2), :]
                 mask = MY[l][k // REP[l]]
                 d = (line(-3, r) - (9.0 * (line(-4, r) + line(-2, r)) - (line(-6, r) + line(0, r))) * 0.0625) * mask
-                dscr[k, 0:r] = d
-                part = lambda s: dscr[k, s : s + n]
+                place = k if l == 0 else 8 * l + (2 * c + a) * half_x + k
+                dscr[place, 0:r] = d
+                part = lambda s: dscr[place, s : s + n]
                 own_part = part(2)
                 smooth = line(0, n) + (9.0 * (part(1) + own_part) - (part(0) + part(3))) * 0.03125
                 to = (c * half_x + k) * n
@@ -212,13 +222,18 @@
                 Y[l][2 * a + 1, h, to : to + n] = own_part
             return carry
 
-        lax.fori_loop(0, ZH[l], body, 0)
-
-    def lift_z(l, ab):
+        if l > 0:
+            body(0, 0)
+        else:
+            lax.fori_loop(0, 2, body, 0)
+
+    def lift_z(l, ab, comps=(0, 1, 2)):
         half_x, n = NX[l] // 2, NY[l] // 2
+        size = half_x * n
+        parts = (ab,) if isinstance(ab, int) else ab
         acc = None
         for h in range(ZH[l]):
-            x = Y[l][ab, h]
+            x = jnp.concatenate([Y[l][ab, h, comps[0] * size : (comps[-1] + 1) * size, :] for ab in parts], axis=0)
             weights = W[l][h * 128 : (h + 1) * 128, :]
             hi = x.astype(BF16)
             rest = x - hi.astype(F32)
@@ -227,14 +242,15 @@
             for piece in (low, mid, hi):
                 term = jnp.dot(piece, weights, preferred_element_type=F32)
                 acc = term if acc is None else acc + term
-        mask = jnp.concatenate([MZ[l][...]] * 3, axis=0)
+        times = len(comps) * len(parts)
+        mask = MZ[l][...] if times == 1 else jnp.concatenate([MZ[l][...]] * times, axis=0)
         smooth = acc[:, :128] + mask * acc[:, 256:]
         detail = mask * acc[:, 128:256]
         lanes = (128, 64, 32)[l]
         out = (o1, o2, o3)[l]
-        for c in range(3):
+        for place, (ab, c) in enumerate([(ab, c) for ab in parts for c in comps]):
             for k in range(half_x):
-                rows = slice((c * half_x + k) * n, (c * half_x + k + 1) * n)
+                rows = slice((place * half_x + k) * n, (place * half_x + k + 1) * n)
                 out[c, 2 * ab, k] = detail[rows, :lanes]
                 if ab > 0:
                     out[c, 2 * ab - 1, k] = smooth[rows, :lanes]
@@ -312,6 +328,7 @@
             lift_x(0, (c,), (t, 0, 1))
             lines[c].append(send_lines(c, 0, t == 3))
     flags_in = send_flags(diagonal)
+    detail_lines = [[send_lines(c, 1, forward) for forward in (True, False)] for c in everything]
     wait_recv(inner)
     vorticity(-6, 0, (1, 2), True)
     vorticity(0, 1, (1, 2), False)
@@ -322,9 +339,8 @@
     for c in everything:
         wait_recv(lines[c])
         lift_y(0, c, 0)
-    lift_z(0, 0)
+        lift_z(0, 0, (c,))
     around2 = send_around(1)
-    lines = [[send_lines(c, 1, forward) for forward in (True, False)] for c in everything]
     wait_recv(flags_in)
     masks(1)
     masks(2)
@@ -337,10 +353,9 @@
     around3 = send_around(2)
     for c in everything:
         lift_y(1, c, 1)
-    for ab in range(1, 4):
-        lift_z(1, ab)
-    for c in everything:
-        wait_recv(lines[c])
+    lift_z(1, (1, 2, 3))
+    for c in everything:
+        wait_recv(detail_lines[c])
         lift_y(0, c, 1)
     lift_z(0, 2)
     lift_z(0, 3)
@@ -349,8 +364,7 @@
     for c in everything:
         for a in range(2):
             lift_y(2, c, a)
-    for ab in range(4):
-        lift_z(2, ab)
+    lift_z(2, (0, 1, 2, 3))
     for copy in pending:
         copy.wait_send()
 
@@ -375,7 +389,7 @@
     scratch += [v((3, ZH[l], NX[l] + 11, NY[l] + 2 * ROWS[l], 128), F32) for l in range(3)]
     scratch += [v((3, ZH[l], 2, NX[l] // 2, NY[l] + 24, 128), F32) for l in range(3)]
     scratch += [v((4, ZH[l], 3 * NX[l] * NY[l] // 4, 128), F32) for l in range(3)]
-    scratch += [v((8, 32, 128), F32), v((9, 3, 2, 4, 128), F32)]
+    scratch += [v((40, 32, 128), F32), v((9, 3, 2, 4, 128), F32)]
     scratch += [v((4 if l < 2 else 5, NY[l] + 2 * ROWS[l], 128), F32) for l in range(3)]
     scratch += [v((2, DR[l], 128), F32) for l in range(3)]
     scratch += [v((NX[l] * NY[l] // 4, 128), F32) for l in range(3)]

time: 46.4 us -> 44.5 us (0.959)
  Pallas kernels: 45.6 us -> 43.7 us
    pallas_call x1, Pallas kernels: 44.3 us -> 42.5 us  [on_device(): pl.pallas_call(kernel, out_shape=[v(shape, F32) for shape in out_shapes],...]
where the time goes in v4:
time: 44.5 us; the launch traced here: 44.4 us
  Pallas kernels  43.7 us (98%)
  between operations  0.64 us (1%)
    pallas_call x1, Pallas kernels, on_device(): pl.pallas_call(kernel, out_shape=[v(shape, F32) for shape in out_shapes],...  42.5 us
    pallas_call x1, Pallas kernels, on_device(): pl.pallas_call(write_out, out_shape=[jax.ShapeDtypeStruct(shape, F32) for...  1.24 us

profile of v4, /device:TPU:1, one launch (start us, length us, event | category | flops | bytes accessed | tf_op | source)
XLA Modules:
  0.0 44.4 jit_solution(1578982427372831024)
XLA Ops:
  0.6 42.5 %analysis.1 = (f32[3,7,8,16,128]{4,3,2,1,0:T(8,128)S(1)}, f32[3,7,4,8,64]{4,3,2,1,0:T(8,128)S(1)}, f32[3,7,2,4,32]{4,3,2,1,0:T(4,128)S(1)}, f32[3,2,4,32]{3,2,1,0:T(4,128)S(1)}) custom-call(f32[3,16,32,256]{3,2,1,0:T(8,128)} %vel_hbm.1, s32[3,2,4]{2,1,0:T(2,128)} %flags.1, f32[3,64]{1,0:T(4,128)} %table.1, s32[16]{0:T(128)} %ix.1, s32[32]{0:T(128)} %iy.1, ...), custom_call_target="tpu_custom_call" | custom-call | tf_op jit(solution)/shard_map/analysis/pallas_call | solution.py:399
  43.1 1.2 %write_out.1 = (f32[3,7,8,16,128]{4,3,2,1,0:T(8,128)}, f32[3,7,4,8,64]{4,3,2,1,0:T(8,128)}, f32[3,7,2,4,32]{4,3,2,1,0:T(4,128)}, f32[3,2,4,32]{3,2,1,0:T(4,128)}) custom-call(f32[3,7,8,16,128]{4,3,2,1,0:T(8,128)S(1)} %get-tuple-element.8.refs_0_, f32[3,7,4,8,64]{4,3,2,1,0:T(8,128)S(1)} %get-tuple-element.9.refs_1_, ...), custom_call_target="tpu_custom_call" | custom-call | tf_op jit(solution)/shard_map/write_out/pallas_call | solution.py:408

commit v5 on v4

--- a/solution.py
+++ b/solution.py
@@ -44,11 +44,11 @@
 
 
 def kernel(
-    vel_hbm, flags, table, ix, iy, iz_ref, w1_hbm, w2_hbm, w3_hbm,
+    vel_hbm, flags_hbm, table_hbm, ix_hbm, iy_hbm, iz_hbm, w1_hbm, w2_hbm, w3_hbm,
     o1, o2, o3, oc,
     vel, hy, c1, c2, c3, x1, x2, x3, y1, y2, y3, dscr,
     mk, mx1, mx2, mx3, my1, my2, my3, mz1, mz2, mz3, mxt, myt, mzt,
-    w1, w2, w3,
+    w1, w2, w3, flags, table, ix, iy, iz_ref,
     send_sem, recv_sem, local_sem,
 ):
     C, X, Y = (c1, c2, c3), (x1, x2, x3), (y1, y2, y3)
@@ -83,6 +83,14 @@
     for step in direct:
         pl.semaphore_signal(barrier, inc=1, device_id=at(*step), device_id_type=pl.DeviceIdType.MESH)
 
+    small = [
+        pltpu.make_async_copy(src, dst, local_sem.at[n])
+        for n, (src, dst) in enumerate(
+            ((flags_hbm, flags), (table_hbm, table), (ix_hbm, ix), (iy_hbm, iy), (iz_hbm, iz_ref)), 4
+        )
+    ]
+    for copy in small:
+        copy.start()
     local = [
         pltpu.make_async_copy(vel_hbm, vel.at[:, pl.ds(7, 16)], local_sem.at[0]),
         pltpu.make_async_copy(w1_hbm, w1, local_sem.at[1]),
@@ -92,6 +100,8 @@
     for copy in local:
         copy.start()
 
+    for copy in small:
+        copy.wait()
     own = slot(0, 0)
     for l in range(3):
         for bx in range(2):
@@ -345,8 +355,14 @@
     masks(1)
     masks(2)
     lift_z(0, 1)
-    wait_recv(around2)
-    lift_x(1, everything, (0, 1, 4))
+    for c in everything:
+        wait_recv(detail_lines[c])
+        lift_y(0, c, 1)
+    lift_z(0, 2)
+    wait_recv(around2[8:12])
+    lift_x(1, everything, (1, 1, 2))
+    wait_recv(around2[:8] + around2[12:])
+    lift_x(1, everything, (0, 3, 2))
     for c in everything:
         lift_y(1, c, 0)
     lift_z(1, 0)
@@ -354,18 +370,18 @@
     for c in everything:
         lift_y(1, c, 1)
     lift_z(1, (1, 2, 3))
-    for c in everything:
-        wait_recv(detail_lines[c])
-        lift_y(0, c, 1)
-    lift_z(0, 2)
     lift_z(0, 3)
-    wait_recv(around3)
-    lift_x(2, everything, (0, 1, 3))
+    for copy in pending[:-14]:
+        copy.wait_send()
+    wait_recv(around3[8:12])
+    lift_x(2, everything, (1, 1, 1))
+    wait_recv(around3[:8] + around3[12:])
+    lift_x(2, everything, (0, 2, 2))
     for c in everything:
         for a in range(2):
             lift_y(2, c, a)
     lift_z(2, (0, 1, 2, 3))
-    for copy in pending:
+    for copy in pending[-14:]:
         copy.wait_send()
 
 
@@ -381,7 +397,6 @@
 def on_device(velocity, refine_flags, metric_table, index_x, index_y, index_z):
     weights = [jnp.asarray(z_matrices(count).astype(np.float32)).astype(BF16) for count in (256, 128, 64)]
     anywhere = pl.BlockSpec(memory_space=pl.ANY)
-    smem = pl.BlockSpec(memory_space=pltpu.SMEM)
     vmem = pl.BlockSpec(memory_space=pltpu.VMEM)
     out_shapes = [(3, 7, 8, 16, 128), (3, 7, 4, 8, 64), (3, 7, 2, 4, 32), (3, 2, 4, 32)]
     v = pltpu.VMEM
@@ -395,11 +410,13 @@
     scratch += [v((NX[l] * NY[l] // 4, 128), F32) for l in range(3)]
     scratch += [v((32, 128), F32), v((32, 128), F32), v((1, 256), F32)]
     scratch += [v((256, 384), BF16), v((128, 384), BF16), v((128, 384), BF16)]
-    scratch += [pltpu.SemaphoreType.DMA((96,)), pltpu.SemaphoreType.DMA((96,)), pltpu.SemaphoreType.DMA((8,))]
+    i32 = jnp.int32
+    scratch += [pltpu.SMEM((3, 2, 4), i32), pltpu.SMEM((3, 64), F32), pltpu.SMEM((16,), i32), pltpu.SMEM((32,), i32), v((1, 256), i32)]
+    scratch += [pltpu.SemaphoreType.DMA((96,)), pltpu.SemaphoreType.DMA((96,)), pltpu.SemaphoreType.DMA((9,))]
     results = pl.pallas_call(
         kernel,
         out_shape=[v(shape, F32) for shape in out_shapes],
-        in_specs=[anywhere, smem, smem, smem, smem, vmem, anywhere, anywhere, anywhere],
+        in_specs=[anywhere] * 9,
         out_specs=[vmem] * 4,
         scratch_shapes=scratch,
         compiler_params=pltpu.CompilerParams(collective_id=0, has_side_effects=True),

time: 44.5 us -> 43.6 us (0.980)
  Pallas kernels: 43.7 us -> 42.8 us
    pallas_call x1, Pallas kernels: 42.5 us -> 41.5 us  [on_device(): pl.pallas_call(kernel, out_shape=[v(shape, F32) for shape in out_shapes],...]
where the time goes in v5:
time: 43.6 us; the launch traced here: 43.4 us
  Pallas kernels  42.8 us (98%)
  between operations  0.64 us (1%)
    pallas_call x1, Pallas kernels, on_device(): pl.pallas_call(kernel, out_shape=[v(shape, F32) for shape in out_shapes],...  41.5 us
    pallas_call x1, Pallas kernels, on_device(): pl.pallas_call(write_out, out_shape=[jax.ShapeDtypeStruct(shape, F32) for...  1.24 us

profile of v5, /device:TPU:1, one launch (start us, length us, event | category | flops | bytes accessed | tf_op | source)
XLA Modules:
  0.0 43.4 jit_solution(18332898196725513882)
XLA Ops:
  0.6 41.5 %analysis.1 = (f32[3,7,8,16,128]{4,3,2,1,0:T(8,128)S(1)}, f32[3,7,4,8,64]{4,3,2,1,0:T(8,128)S(1)}, f32[3,7,2,4,32]{4,3,2,1,0:T(4,128)S(1)}, f32[3,2,4,32]{3,2,1,0:T(4,128)S(1)}) custom-call(f32[3,16,32,256]{3,2,1,0:T(8,128)} %vel_hbm.1, s32[3,2,4]{2,1,0:T(2,128)} %flags_hbm.1, f32[3,64]{1,0:T(4,128)} %table_hbm.1, s32[16]{0:T(128)} %ix_hbm.1, s32[32]{0:T(128)} %iy_hbm.1, ...), custom_call_target="tpu_custom_call" | custom-call | tf_op jit(solution)/shard_map/analysis/pallas_call | solution.py:416
  42.2 1.2 %write_out.1 = (f32[3,7,8,16,128]{4,3,2,1,0:T(8,128)}, f32[3,7,4,8,64]{4,3,2,1,0:T(8,128)}, f32[3,7,2,4,32]{4,3,2,1,0:T(4,128)}, f32[3,2,4,32]{3,2,1,0:T(4,128)}) custom-call(f32[3,7,8,16,128]{4,3,2,1,0:T(8,128)S(1)} %get-tuple-element.8.refs_0_, f32[3,7,4,8,64]{4,3,2,1,0:T(8,128)S(1)} %get-tuple-element.9.refs_1_, ...), custom_call_target="tpu_custom_call" | custom-call | tf_op jit(solution)/shard_map/write_out/pallas_call | solution.py:425
